TPU v7x, 32 devices: a whole 2x2x4 slice. The times are simulated.
32 devices in a mesh: wide: 8 (over y, x, core), narrow: 4 (over z).
Axes of the slice: x: 2, y: 2, z: 4, core: 2. Of those that a mesh axis runs over, the one named last changes fastest.
Arguments:
- features: bfloat16 [131072, 512], P(('wide', 'narrow')), may hold values from -6 to 6
- adjacency: bfloat16 [3072, 128, 128], P(('wide', 'narrow')), may hold values from -0.375 to 0.375
- block_rows: int32 [32, 96], P(('wide', 'narrow')), may hold values from 0 to 31, as said below
- block_cols: int32 [32, 96], P(('wide', 'narrow')), may hold values from 0 to 39, as said below
- block_count: int32 [32], P(('wide', 'narrow')), may hold values from 40 to 96, as said below
- node_count: int32 [32], P(('wide', 'narrow')), may hold values from 2048 to 4096, as said below
- halo_index: int32 [32, 4, 256], P(('wide', 'narrow')), may hold values from 0 to 2047, as said below
- weight: bfloat16 [512, 512], replicated, may hold values from -0.25 to 0.25
- bias: float32 [512], replicated, may hold values from -3 to 3
- out_grad: bfloat16 [131072, 512], P(('wide', 'narrow')), may hold values from -6 to 6
Outputs:
- output: bfloat16 [131072, 512], P(('wide', 'narrow'))
- input_grad: bfloat16 [131072, 512], P(('wide', 'narrow'))
- weight_grad: float32 [512, 512], replicated
- bias_grad: float32 [512], replicated
Inputs may be any that keep to these rules, and one draw needn't show every extreme that they name: `block_count`: each device's live slots include every one of its 32 diagonal blocks and every one of its 8 halo column blocks at least once; some device has all 96 slots live. `block_rows`: within range for live and non-live slots. `block_cols`: within range for live and non-live slots. `node_count`: some device has all 4096 slots live. `halo_index`: the 1024 rows of one device are distinct and all live.
All inputs are finite; a program needn't handle non-finite values.
Results may differ from a plain program's by a relative error of at most 0.0062.
Values may be sent and summed in bfloat16 or wider, within the bound.
A program may use at most 192 MiB of HBM per device.

v0:
```python
import functools
import math

import jax
import jax.numpy as jnp
from jax import lax
from jax.experimental import pallas as pl
from jax.experimental.pallas import tpu as pltpu
from jax.sharding import PartitionSpec as P

MESH = pl.DeviceIdType.MESH
ANY = pl.ANY
VMEM_LIMIT = 60 * 1024 * 1024


def neighbours(n_wide, n_narrow):
    w = lax.axis_index("wide")
    n = lax.axis_index("narrow")
    return (
        (w > 0, (w - 1, n)),
        (w < n_wide - 1, (w + 1, n)),
        (n > 0, (w, n - 1)),
        (n < n_narrow - 1, (w, n + 1)),
    )


def halo_copy(src, dst, send, recv, k, target):
    return pltpu.make_async_remote_copy(
        src_ref=src.at[k],
        dst_ref=dst.at[k ^ 1],
        send_sem=send.at[k],
        recv_sem=recv.at[k ^ 1],
        device_id=target,
        device_id_type=MESH,
    )


def tables(row_ref, col_ref, pads, count, row_blocks, col_blocks):
    lanes = pads.shape[1]
    slots = row_ref.shape[1]
    f32 = jnp.float32
    pads[...] = jnp.zeros_like(pads)
    pads[0:1, 0:slots] = row_ref[...]
    pads[1:2, 0:slots] = col_ref[...]
    lane = lax.broadcasted_iota(jnp.int32, (lanes, lanes), 1).astype(f32)
    sub = lax.broadcasted_iota(jnp.int32, (lanes, lanes), 0).astype(f32)

    def spread(x):
        return jnp.broadcast_to(x.astype(f32), (lanes, lanes))

    halo_blocks = col_blocks - row_blocks
    col = spread(pads[1:2, :])
    place = jnp.where(col >= row_blocks, col - row_blocks, col + halo_blocks)
    place = jnp.where(lane < count.astype(f32), place, float(col_blocks))
    place_t = jnp.transpose(place)
    row_t = jnp.transpose(spread(pads[0:1, :]))
    same = place == place_t
    ahead = lane < sub
    one = lambda m: jnp.where(m, 1.0, 0.0)
    rank = jnp.sum(one((place < place_t) | (same & ahead)), 1, keepdims=True)
    twin = jnp.minimum(jnp.sum(one(same & ahead), 1, keepdims=True), 1.0)
    hot = one(jnp.broadcast_to(rank, (lanes, lanes)) == lane)
    pick = lambda x: jnp.sum(hot * x, 0, keepdims=True)
    ends = jnp.sum(one(place_t <= lane), 0, keepdims=True)
    keep = pick(jnp.broadcast_to(twin, (lanes, lanes)))
    return pick(sub), pick(row_t), keep, ends


def gather_kernel(
    n_wide,
    n_narrow,
    row_blocks,
    col_blocks,
    idx_ref,
    row_ref,
    col_ref,
    count_ref,
    feat_hbm,
    halo_ref,
    table_ref,
    pads,
    feat,
    packed,
    load,
    send,
    recv,
):
    count = idx_ref.shape[2]
    span = feat.shape[0]
    fetch = pltpu.make_async_copy(feat_hbm.at[pl.ds(0, span)], feat, load)
    fetch.start()
    near = neighbours(n_wide, n_narrow)
    barrier = pltpu.get_barrier_semaphore()
    for there, target in near:

        @pl.when(there)
        def _():
            pl.semaphore_signal(barrier, inc=1, device_id=target, device_id_type=MESH)

    fetch.wait()
    lane = lax.broadcasted_iota(jnp.int32, (count, 128), 1).astype(jnp.float32)

    def pack(k):
        row = idx_ref[0, pl.ds(k, 1), :].astype(jnp.float32)
        column = jnp.transpose(jnp.broadcast_to(row, (128, count)))
        hot = jnp.concatenate(
            [
                jnp.where(column == lane + float(at), 1.0, 0.0).astype(jnp.bfloat16)
                for at in range(0, span, 128)
            ],
            axis=1,
        )
        packed[k] = jnp.dot(hot, feat[...], preferred_element_type=jnp.float32).astype(
            jnp.bfloat16
        )

    pack(2)
    pl.semaphore_wait(barrier, sum(there.astype(jnp.int32) for there, _ in near))
    for k in (2, 3, 1, 0):
        there, target = near[k]
        if k != 2:
            pack(k)

        @pl.when(there)
        def _():
            halo_copy(packed, halo_ref, send, recv, k, target).start()

        @pl.when(jnp.logical_not(there))
        def _():
            halo_ref[k] = jnp.zeros(halo_ref.shape[1:], halo_ref.dtype)

    table_ref[...] = jnp.zeros_like(table_ref)
    for i, line in enumerate(
        tables(row_ref, col_ref, pads, count_ref[0], row_blocks, col_blocks)
    ):
        table_ref[pl.ds(i, 1), :] = line.astype(jnp.int32)

    for k in range(4):
        there, target = near[k]

        @pl.when(there)
        def _():
            halo_copy(packed, halo_ref, send, recv, k, target).wait_send()
            halo_copy(packed, halo_ref, send, recv, k ^ 1, target).wait_recv()


def layer_kernel(
    step,
    rows,
    cols,
    live,
    nodes_live,
    feat_hbm,
    halo_hbm,
    adj_hbm,
    grad_hbm,
    w_ref,
    b_ref,
    out_hbm,
    back_hbm,
    wg_ref,
    bg_ref,
    ext,
    adj,
    grad,
    acc,
    back,
    out,
    wsum,
    bsum,
    sem,
    out_sem,
    back_sem,
):
    row_blocks, side, width = feat_hbm.shape
    halo_blocks = halo_hbm.shape[0]
    count = live[0]
    keep_to = nodes_live[0]
    loads = [
        pltpu.make_async_copy(feat_hbm, ext.at[pl.ds(0, row_blocks)], sem.at[0]),
        pltpu.make_async_copy(halo_hbm, ext.at[pl.ds(row_blocks, halo_blocks)], sem.at[1]),
        pltpu.make_async_copy(adj_hbm, adj, sem.at[2]),
        pltpu.make_async_copy(grad_hbm, grad, sem.at[3]),
    ]
    for load in loads[:3]:
        load.start()

    def clear(i, carry):
        acc[i] = jnp.zeros((side, width), jnp.float32)
        return carry

    lax.fori_loop(0, row_blocks + 1, clear, 0)
    wsum[...] = jnp.zeros_like(wsum)
    bsum[...] = jnp.zeros_like(bsum)
    for load in loads[:3]:
        load.wait()
    loads[3].start()

    def kept(block, blocks=1):
        at = lax.broadcasted_iota(jnp.int32, (blocks * side, width), 0)
        return at < keep_to - block * side

    def mask(i, carry):
        ext[i] = jnp.where(kept(i), ext[i].astype(jnp.float32), 0.0).astype(ext.dtype)
        return carry

    lax.fori_loop(keep_to // side, row_blocks, mask, 0)

    unroll = 16
    trips = (count + unroll - 1) // unroll

    def forward(t, carry):
        for u in range(unroll):
            b = t * unroll + u
            to = jnp.where(b < count, rows[b], row_blocks)
            acc[to] += jnp.dot(adj[b], ext[cols[b]], preferred_element_type=jnp.float32)
        return carry

    lax.fori_loop(0, trips, forward, 0)
    loads[3].wait()

    def put(i):
        return pltpu.make_async_copy(
            out.at[pl.ds(i * step, step)], out_hbm.at[pl.ds(i * step, step)], out_sem.at[i]
        )

    def put_back(i):
        return pltpu.make_async_copy(
            back.at[pl.ds(i * step, step)], back_hbm.at[pl.ds(i * step, step)], back_sem.at[i]
        )

    tall = step * side

    def into(i):
        at = pl.ds(i * step, step)
        agg = acc[at].reshape(tall, width).astype(jnp.bfloat16)
        return agg, jnp.dot(agg, w_ref[...], preferred_element_type=jnp.float32)

    def middle(i, pre):
        at = pl.ds(i * step, step)
        pre = pre + b_ref[...]
        keep = kept(i * step, step)
        sig = 0.5 * jnp.tanh(0.5 * pre) + 0.5
        act = pre * sig
        out[at] = jnp.where(keep, act, 0.0).astype(jnp.bfloat16).reshape(step, side, width)
        put(i).start()
        g = grad[at].reshape(tall, width).astype(jnp.float32)
        dpre = jnp.where(keep, g * (sig + act * (1.0 - sig)), 0.0).astype(jnp.bfloat16)
        bsum[...] += jnp.sum(dpre.astype(jnp.float32).reshape(tall // 8, 8, width), 0)
        return dpre

    def after(i, agg, dpre):
        wsum[...] += lax.dot_general(
            agg, dpre, (((0,), (0,)), ((), ())), preferred_element_type=jnp.float32
        )
        back[pl.ds(i * step, step)] = (
            lax.dot_general(
                dpre, w_ref[...], (((1,), (1,)), ((), ())), preferred_element_type=jnp.float32
            )
            .astype(jnp.bfloat16)
            .reshape(step, side, width)
        )
        put_back(i).start()

    group = 8

    def dense(t, carry):
        now = into(t * group)
        for u in range(group):
            i = t * group + u
            later = into(i + 1) if u + 1 < group else None
            dpre = middle(i, now[1])
            after(i, now[0], dpre)
            now = later
        return carry

    lax.fori_loop(0, row_blocks // step // group, dense, 0)
    wg_ref[...] = wsum[...].astype(wg_ref.dtype)
    bg_ref[...] = jnp.sum(bsum[...], 0, keepdims=True)

    def drain(i, carry):
        put(i).wait()
        put_back(i).wait()
        return carry

    lax.fori_loop(0, row_blocks // step, drain, 0)


def back_kernel(
    n_wide,
    n_narrow,
    scale,
    table,
    nodes_live,
    idx_ref,
    wg_ref,
    bg_ref,
    adj_hbm,
    back_hbm,
    grad_hbm,
    wout_ref,
    bout_ref,
    grad_ref,
    grad_sem,
    adj,
    back,
    run,
    ret,
    incoming,
    rs_wide,
    rs_narrow,
    part,
    ag_narrow,
    ag_wide,
    b_wide,
    b_mid,
    b_narrow,
    load,
    send,
    recv,
    send_w,
    recv_w,
    send_n,
    recv_n,
    send_gn,
    recv_gn,
    send_gw,
    recv_gw,
    send_bw,
    recv_bw,
    send_bn,
    recv_bn,
):
    w = lax.axis_index("wide")
    n = lax.axis_index("narrow")
    slab = wg_ref.shape[1]
    part_width = rs_narrow.shape[2]
    row_blocks, side, width = back.shape
    slots = adj.shape[0]
    loads = [
        pltpu.make_async_copy(back_hbm, back, load.at[0]),
        pltpu.make_async_copy(adj_hbm, adj, load.at[1]),
    ]
    for fetch in loads:
        fetch.start()

    def wide_peer(d):
        return (lax.rem(w + d, n_wide), n)

    def narrow_peer(d):
        return (w, lax.rem(n + d, n_narrow))

    peers = [wide_peer(d) for d in range(1, n_wide)] + [
        narrow_peer(d) for d in range(1, n_narrow)
    ]
    barrier = pltpu.get_barrier_semaphore()
    for peer in peers:
        pl.semaphore_signal(barrier, inc=1, device_id=peer, device_id_type=MESH)
    pl.semaphore_wait(barrier, len(peers))

    def remote(src, dst, s, r, peer):
        return pltpu.make_async_remote_copy(
            src_ref=src, dst_ref=dst, send_sem=s, recv_sem=r, device_id=peer, device_id_type=MESH
        )

    pending = []
    near = neighbours(n_wide, n_narrow)

    first = []
    for d in range(1, n_wide):
        peer = wide_peer(d)
        c = remote(wg_ref.at[peer[0]], rs_wide.at[d], send_w.at[d], recv_w.at[d], peer)
        c.start()
        first.append(c)
    bias_first = []
    for d in range(1, n_wide):
        c = remote(bg_ref, b_wide.at[d], send_bw.at[d], recv_bw.at[d], wide_peer(d))
        c.start()
        bias_first.append(c)
    run[0] = jnp.zeros(run.shape[1:], run.dtype)
    for fetch in loads:
        fetch.wait()
    unroll = 16

    def backward(t, carry):
        held = run[t * unroll]
        for u in range(unroll):
            k = t * unroll + u
            held = held * table[2, k].astype(jnp.float32) + lax.dot_general(
                adj[table[0, k]],
                back[table[1, k]],
                (((0,), (0,)), ((), ())),
                preferred_element_type=jnp.float32,
            )
            run[k + 1] = held
        return carry

    early = (slots - row_blocks) // unroll
    lax.fori_loop(0, early, backward, 0)
    halo_blocks = ret.shape[0] * ret.shape[1] // side
    per = ret.shape[1] // side
    for k in (2, 3, 1, 0):
        there, target = near[k]
        for j in range(per):
            ret[k, pl.ds(j * side, side), :] = run[table[3, k * per + j]].astype(ret.dtype)

        @pl.when(there)
        def _():
            halo_copy(ret, incoming, send, recv, k, target).start()

        @pl.when(jnp.logical_not(there))
        def _():
            incoming[k] = jnp.zeros(incoming.shape[1:], incoming.dtype)

    total = wg_ref[w].astype(jnp.float32)
    for c in first:
        c.wait_recv()
    for d in range(1, n_wide):
        total = total + rs_wide[d].astype(jnp.float32)
    bias = bg_ref[...]
    for c in bias_first:
        c.wait_recv()
    for d in range(1, n_wide):
        bias = bias + b_wide[d]
    b_mid[...] = bias
    for j in range(n_narrow):
        part[j] = total[:, j * part_width : (j + 1) * part_width].astype(part.dtype)
    second = []
    for d in range(1, n_narrow):
        peer = narrow_peer(d)
        c = remote(part.at[peer[1]], rs_narrow.at[d], send_n.at[d], recv_n.at[d], peer)
        c.start()
        second.append(c)
    for d in range(1, n_narrow):
        c = remote(b_mid, b_narrow.at[d], send_bn.at[d], recv_bn.at[d], narrow_peer(d))
        c.start()
        bias_first.append(c)
        second.append(c)
    lax.fori_loop(early, slots // unroll, backward, 0)
    piece = part[n].astype(jnp.float32)
    for c in second:
        c.wait_recv()
    for d in range(1, n_narrow):
        piece = piece + rs_narrow[d].astype(jnp.float32)
        bias = bias + b_narrow[d]
    bout_ref[...] = bias * scale
    ag_narrow[n] = (piece * scale).astype(ag_narrow.dtype)
    third = []
    for d in range(1, n_narrow):
        c = remote(
            ag_narrow.at[n], ag_narrow.at[n], send_gn.at[d], recv_gn.at[d], narrow_peer(d)
        )
        c.start()
        third.append(c)
    chunk = grad_ref.shape[1]
    across = chunk // side
    keep_to = nodes_live[0]

    def own(i):
        return jnp.concatenate(
            [run[table[3, halo_blocks + i * across + j]] for j in range(across)], 0
        )

    def leave(i):
        return pltpu.make_async_copy(grad_ref.at[i], grad_hbm.at[i], grad_sem.at[i])

    def finish(i, full):
        row = lax.broadcasted_iota(jnp.int32, full.shape, 0) + i * chunk
        grad_ref[i] = jnp.where(row < keep_to, full, 0.0).astype(grad_ref.dtype)
        leave(i).start()

    low_chunks = row_blocks // across // 2

    def high(i, carry):
        finish(i, own(i))
        return carry

    lax.fori_loop(low_chunks, row_blocks // across, high, 0)
    for c in third:
        c.wait_recv()
    fourth = []
    for d in range(1, n_wide):
        c = remote(ag_narrow, ag_wide.at[w], send_gw.at[d], recv_gw.at[d], wide_peer(d))
        c.start()
        fourth.append(c)
    ag_wide[w] = ag_narrow[...]

    for k in range(4):
        there, target = near[k]

        @pl.when(there)
        def _():
            halo_copy(ret, incoming, send, recv, k, target).wait_send()
            halo_copy(ret, incoming, send, recv, k ^ 1, target).wait_recv()

    merged = incoming[...].reshape(-1, width)
    idx = jnp.concatenate([idx_ref[0, k : k + 1, :] for k in range(4)], 1)

    def scatter(i, carry):
        at = lax.broadcasted_iota(jnp.int32, (chunk, idx.shape[1]), 0) + i * chunk
        hot = jnp.where(at == idx, 1.0, 0.0).astype(jnp.bfloat16)
        finish(i, own(i) + jnp.dot(hot, merged, preferred_element_type=jnp.float32))
        return carry

    lax.fori_loop(0, low_chunks, scatter, 0)
    for c in fourth:
        c.wait_recv()
    for i in range(n_wide):
        for j in range(n_narrow):
            wout_ref[pl.ds(i * slab, slab), pl.ds(j * part_width, part_width)] = ag_wide[
                i, j
            ].astype(jnp.float32)
    def drain(i, carry):
        leave(i).wait()
        return carry

    lax.fori_loop(0, row_blocks // across, drain, 0)
    for c in first + bias_first + second[: n_narrow - 1] + third + fourth:
        c.wait_send()


def hand_on(grad_in, w_in, b_in, grad_out, w_out, b_out, grad, wg, bg, take, give):
    pieces = grad.shape[0]
    hops = [(grad_in.at[i], grad.at[i], grad_out.at[i]) for i in range(pieces)]
    hops += [(w_in, wg, w_out), (b_in, bg, b_out)]
    ins = [pltpu.make_async_copy(a, b, take.at[i]) for i, (a, b, _) in enumerate(hops)]
    outs = [pltpu.make_async_copy(b, c, give.at[i]) for i, (_, b, c) in enumerate(hops)]
    for c in ins:
        c.start()
    for c, d in zip(ins, outs):
        c.wait()
        d.start()
    for d in outs:
        d.wait()


def local(
    n_wide,
    n_narrow,
    features,
    adjacency,
    block_rows,
    block_cols,
    block_count,
    node_count,
    halo_index,
    weight,
    bias,
    out_grad,
):
    nodes, width = features.shape
    slots, side, _ = adjacency.shape
    row_blocks = nodes // side
    sides, halo = halo_index.shape[1:]
    halo_blocks = sides * halo // side
    col_blocks = row_blocks + halo_blocks
    bf, f32 = jnp.bfloat16, jnp.float32
    vm = pl.BlockSpec(memory_space=pltpu.VMEM)
    sm = pl.BlockSpec(memory_space=pltpu.SMEM)
    hb = pl.BlockSpec(memory_space=ANY)
    dma = pltpu.SemaphoreType.DMA

    lanes = -(-slots // 128) * 128
    halos, table = pl.pallas_call(
        functools.partial(gather_kernel, n_wide, n_narrow, row_blocks, col_blocks),
        name="halo_out",
        out_shape=(
            jax.ShapeDtypeStruct((sides, halo, width), bf),
            jax.ShapeDtypeStruct((8, lanes), jnp.int32),
        ),
        in_specs=[vm, vm, vm, sm, hb],
        out_specs=(vm, vm),
        scratch_shapes=[
            pltpu.VMEM((8, lanes), jnp.int32),
            pltpu.VMEM((nodes // 2, width), bf),
            pltpu.VMEM((sides, halo, width), bf),
            dma,
            dma((sides,)),
            dma((sides,)),
        ],
        compiler_params=pltpu.CompilerParams(
            collective_id=0, has_side_effects=True, vmem_limit_bytes=VMEM_LIMIT
        ),
    )(
        halo_index,
        block_rows,
        block_cols,
        block_count,
        features,
    )

    step = 2
    blocked = (row_blocks, side, width)
    out, back, wg, bg = pl.pallas_call(
        functools.partial(layer_kernel, step),
        name="layer",
        out_shape=(
            jax.ShapeDtypeStruct(blocked, bf),
            jax.ShapeDtypeStruct(blocked, bf),
            jax.ShapeDtypeStruct((width, width), bf),
            jax.ShapeDtypeStruct((1, width), f32),
        ),
        in_specs=[sm, sm, sm, sm, hb, hb, hb, hb, vm, vm],
        out_specs=(hb, hb, vm, vm),
        scratch_shapes=[
            pltpu.VMEM((col_blocks, side, width), bf),
            pltpu.VMEM((slots, side, side), bf),
            pltpu.VMEM(blocked, bf),
            pltpu.VMEM((row_blocks + 1, side, width), f32),
            pltpu.VMEM(blocked, bf),
            pltpu.VMEM(blocked, bf),
            pltpu.VMEM((width, width), f32),
            pltpu.VMEM((8, width), f32),
            dma((4,)),
            dma((row_blocks // step,)),
            dma((row_blocks // step,)),
        ],
        compiler_params=pltpu.CompilerParams(vmem_limit_bytes=VMEM_LIMIT),
    )(
        block_rows[0],
        block_cols[0],
        block_count,
        node_count,
        features.reshape(blocked),
        halos.reshape(halo_blocks, side, width),
        adjacency,
        out_grad.reshape(blocked),
        weight,
        bias.reshape(1, width),
    )

    slab = width // n_wide
    part_width = width // n_narrow
    scale = 1.0 / math.sqrt(nodes * n_wide * n_narrow)
    chunk = 2 * side
    input_grad, wout, bout = pl.pallas_call(
        functools.partial(back_kernel, n_wide, n_narrow, scale),
        name="back",
        out_shape=(
            jax.ShapeDtypeStruct((nodes // chunk, chunk, width), bf),
            jax.ShapeDtypeStruct((width, width), f32),
            jax.ShapeDtypeStruct((1, width), f32),
        ),
        in_specs=[sm, sm, vm, vm, vm, hb, hb],
        out_specs=(hb, vm, vm),
        scratch_shapes=[
            pltpu.VMEM((nodes // chunk, chunk, width), bf),
            dma((nodes // chunk,)),
            pltpu.VMEM((slots, side, side), bf),
            pltpu.VMEM(blocked, bf),
            pltpu.VMEM((slots + 1, side, width), f32),
            pltpu.VMEM((sides, halo, width), bf),
            pltpu.VMEM((sides, halo, width), bf),
            pltpu.VMEM((n_wide, slab, width), bf),
            pltpu.VMEM((n_narrow, slab, part_width), bf),
            pltpu.VMEM((n_narrow, slab, part_width), bf),
            pltpu.VMEM((n_narrow, slab, part_width), bf),
            pltpu.VMEM((n_wide, n_narrow, slab, part_width), bf),
            pltpu.VMEM((n_wide, 1, width), f32),
            pltpu.VMEM((1, width), f32),
            pltpu.VMEM((n_narrow, 1, width), f32),
            dma((2,)),
            dma((sides,)),
            dma((sides,)),
        ]
        + [dma((n_wide,))] * 2
        + [dma((n_narrow,))] * 4
        + [dma((n_wide,))] * 4
        + [dma((n_narrow,))] * 2,
        compiler_params=pltpu.CompilerParams(
            collective_id=1, has_side_effects=True, vmem_limit_bytes=VMEM_LIMIT
        ),
    )(
        table,
        node_count,
        halo_index,
        wg.reshape(n_wide, slab, width),
        bg,
        adjacency,
        back,
    )
    pieces = 8
    input_grad, wout, bout = pl.pallas_call(
        hand_on,
        name="hand_on",
        out_shape=(
            jax.ShapeDtypeStruct((pieces, nodes // pieces, width), bf),
            jax.ShapeDtypeStruct((width, width), f32),
            jax.ShapeDtypeStruct((1, width), f32),
        ),
        in_specs=[hb, hb, hb],
        out_specs=(hb, hb, hb),
        scratch_shapes=[
            pltpu.VMEM((pieces, nodes // pieces, width), bf),
            pltpu.VMEM((width, width), f32),
            pltpu.VMEM((1, width), f32),
            dma((pieces + 2,)),
            dma((pieces + 2,)),
        ],
        compiler_params=pltpu.CompilerParams(vmem_limit_bytes=VMEM_LIMIT),
    )(input_grad.reshape(pieces, nodes // pieces, width), wout, bout)
    return out.reshape(nodes, width), input_grad.reshape(nodes, width), wout, bout.reshape(width)


def solution(mesh):
    both = ("wide", "narrow")
    placed = (
        P(both, None),
        P(both, None, None),
        P(both, None),
        P(both, None),
        P(both),
        P(both),
        P(both, None, None),
        P(),
        P(),
        P(both, None),
    )
    return jax.shard_map(
        functools.partial(local, mesh.shape["wide"], mesh.shape["narrow"]),
        mesh=mesh,
        in_specs=placed,
        out_specs=(P(both, None), P(both, None), P(), P()),
        check_vma=False,
    )
```

profile of v0, /device:TPU:0, one launch (start us, length us, event | category | flops | bytes accessed | tf_op | source)
XLA Modules:
  0.0 73.4 jit_solution(18181831227024638913)
XLA Ops:
  1.9 13.5 %halo_out.1 = (bf16[4,256,512]{2,1,0:T(8,128)(2,1)}, s32[8,128]{1,0:T(8,128)}) custom-call(s32[1,4,256]{2,1,0:T(4,128)} %idx_ref.3, s32[1,96]{1,0:T(1,128)} %row_ref.1, s32[1,96]{1,0:T(1,128)} %col_ref.1, s32[1]{0:T(128)S(6)} %copy.14.count_ref.live, bf16[4096,512]{1,0:T(8,128)(2,1)} %feat_hbm.1), custom_call_target="tpu_custom_call" | custom-call | tf_op jit(solution)/shard_map/halo_out/pallas_call | solution.py:564
  15.4 21.8 %layer.1 = (bf16[32,128,512]{2,1,0:T(8,128)(2,1)}, bf16[32,128,512]{2,1,0:T(8,128)(2,1)}, bf16[512,512]{1,0:T(8,128)(2,1)}, f32[1,512]{1,0:T(1,128)}) custom-call(s32[96]{0:T(128)} %bitcast.17, s32[96]{0:T(128)} %bitcast.18, s32[1]{0:T(128)S(6)} %copy.14.count_ref.live, s32[1]{0:T(128)S(6)} %copy.15.nodes_live, bf16[32,128,512]{2,1,0:T(8,128)(2,1)} %bitcast.11, ...), custom_call_target="tpu_custom_call" | custom-call | tf_op jit(solution)/shard_map/layer/pallas_call | solution.py:594
  37.2 31.3 %back.1 = (bf16[16,256,512]{2,1,0:T(8,128)(2,1)}, f32[512,512]{1,0:T(8,128)}, f32[1,512]{1,0:T(1,128)}) custom-call(s32[8,128]{1,0:T(8,128)} %get-tuple-element.18.table, s32[1]{0:T(128)S(6)} %copy.15.nodes_live, s32[1,4,256]{2,1,0:T(4,128)} %idx_ref.3, bf16[8,64,512]{2,1,0:T(8,128)(2,1)} %bitcast.15, f32[1,512]{1,0:T(1,128)} %get-tuple-element.20.bg_ref, ...), custom_call_target="tpu_custom_call" | custom-call | tf_op jit(solution)/shard_map/back/pallas_call | solution.py:636
  68.5 4.9 %hand_on.1 = (bf16[8,512,512]{2,1,0:T(8,128)(2,1)}, f32[512,512]{1,0:T(8,128)}, f32[1,512]{1,0:T(1,128)}) custom-call(bf16[8,512,512]{2,1,0:T(8,128)(2,1)} %bitcast.12, f32[512,512]{1,0:T(8,128)} %get-tuple-element.23.w_in, f32[1,512]{1,0:T(1,128)} %get-tuple-element.24.b_in), custom_call_target="tpu_custom_call" | custom-call | tf_op jit(solution)/shard_map/hand_on/pallas_call | solution.py:683
where the time goes:
time: 73.3 us; the launch traced here: 73.4 us
  Pallas kernels  71.5 us (98%)
  between operations  1.95 us (3%)
    pallas_call x1, Pallas kernels, local(): pl.pallas_call(functools.partial(back_kernel, n_wide, n_narrow, scale), n...  31.3 us
    pallas_call x1, Pallas kernels, local(): pl.pallas_call(functools.partial(layer_kernel, step), name='layer', out_s...  21.8 us
    pallas_call x1, Pallas kernels, local(): pl.pallas_call(functools.partial(gather_kernel, n_wide, n_narrow, row_blo...  13.5 us
    pallas_call x1, Pallas kernels, local(): pl.pallas_call(hand_on, name='hand_on', out_shape=(jax.ShapeDtypeStruct((...  4.92 us

commit v1 on v0

v1 whole, which is shorter than its diff:
```python
import functools
import math

import jax
import jax.numpy as jnp
from jax import lax
from jax.experimental import pallas as pl
from jax.experimental.pallas import tpu as pltpu
from jax.sharding import PartitionSpec as P

MESH = pl.DeviceIdType.MESH
ANY = pl.ANY
VMEM_LIMIT = 60 * 1024 * 1024
FINISH_LIMIT = 60 * 1024 * 1024
BF = jnp.bfloat16
F32 = jnp.float32


def neighbours(n_wide, n_narrow):
    w = lax.axis_index("wide")
    n = lax.axis_index("narrow")
    return (
        (w > 0, (w - 1, n)),
        (w < n_wide - 1, (w + 1, n)),
        (n > 0, (w, n - 1)),
        (n < n_narrow - 1, (w, n + 1)),
    )


def halo_copy(src, dst, send, recv, k, target):
    return pltpu.make_async_remote_copy(
        src_ref=src.at[k],
        dst_ref=dst.at[k ^ 1],
        send_sem=send.at[k],
        recv_sem=recv.at[k ^ 1],
        device_id=target,
        device_id_type=MESH,
    )


def tables(row_ref, col_ref, pads, count, row_blocks, col_blocks):
    lanes = pads.shape[1]
    slots = row_ref.shape[1]
    halo_blocks = col_blocks - row_blocks
    pads[...] = jnp.zeros(pads.shape, pads.dtype)
    pads[0:1, 0:slots] = row_ref[...]
    pads[1:2, 0:slots] = col_ref[...]
    lane = lax.broadcasted_iota(jnp.int32, (lanes, lanes), 1)
    sub = lax.broadcasted_iota(jnp.int32, (lanes, lanes), 0)
    one = lambda m: jnp.where(m, 1, 0)
    spread = lambda x: jnp.broadcast_to(x, (lanes, lanes))
    down = lambda x: jnp.sum(x, 0, keepdims=True)
    across = lambda x: jnp.sum(x, 1, keepdims=True)

    row, col = spread(pads[0:1, :]), spread(pads[1:2, :])
    row_t, col_t = jnp.transpose(row), jnp.transpose(col)
    live = lane < count
    own = live & (col < row_blocks)
    own_t = (sub < count) & (col_t < row_blocks)
    before = own_t & (sub < lane)

    def first(a, a_t):
        return own & (spread(down(one(before & (a_t == a)))) == 0)

    def order(key):
        key_t = jnp.transpose(key)
        same = (key == key_t) & (lane < sub)
        rank = across(one((key < key_t) | same))
        twin = jnp.minimum(across(one(same)), 1)
        hot = one(jnp.broadcast_to(rank, (lanes, lanes)) == lane)
        return key_t, rank, twin, lambda x: down(hot * x)

    dead = 2 * col_blocks
    lead = first(row, row_t)
    key_t, rank, twin, pick = order(
        jnp.where(lead, row, jnp.where(live, row + row_blocks, dead))
    )
    at = lane + row_blocks
    has = down(one(key_t == at))
    last = jnp.where(has > 0, down(one(key_t <= at)) - 1, lane[0:1, :])
    prev = jnp.where(twin > 0, rank - 1, row_t)
    lines = [pick(sub), pick(col_t), pick(prev), last]

    lead = first(col, col_t)
    own_key = jnp.where(lead, col + (col_blocks + 1), col + halo_blocks)
    key = jnp.where(col < row_blocks, own_key, col - row_blocks)
    unused = jnp.where(lane < slots, col_blocks, dead)
    key_t, rank, twin, pick = order(jnp.where(live, key, unused))
    has = down(one(key_t == lane))
    ends = jnp.where(has > 0, down(one(key_t <= lane)), 0)
    keep = pick(jnp.broadcast_to(twin, (lanes, lanes)))
    lines += [pick(sub), pick(row_t), keep, ends]
    slot, block = slots - 1, row_blocks - 1
    tops = (slot, col_blocks - 1, slot, slot, slot, block, 1, slots - row_blocks)
    return [jnp.clip(line, 0, top) for line, top in zip(lines, tops)]


def layer_kernel(
    n_wide,
    n_narrow,
    scale,
    step,
    idx_ref,
    row_ref,
    col_ref,
    live,
    nodes_live,
    b_ref,
    feat_hbm,
    adj_hbm,
    grad_hbm,
    w_hbm,
    out_hbm,
    spread_hbm,
    incoming_hbm,
    wout_hbm,
    bout_hbm,
    grad,
    own_spread,
    incoming,
    wout_ref,
    bout_ref,
    pads,
    lined,
    table,
    ext,
    adj,
    w_ref,
    run,
    packed,
    landing,
    ret,
    wsum,
    wg,
    bsum,
    bg,
    rs_wide,
    rs_narrow,
    part,
    ag_narrow,
    ag_wide,
    b_wide,
    b_mid,
    b_narrow,
    load,
    out_sem,
    own_sem,
    give,
    send,
    recv,
    send_r,
    recv_r,
    send_w,
    recv_w,
    send_n,
    recv_n,
    send_gn,
    recv_gn,
    send_gw,
    recv_gw,
    send_bw,
    recv_bw,
    send_bn,
    recv_bn,
):
    w = lax.axis_index("wide")
    n = lax.axis_index("narrow")
    slots = adj.shape[0]
    row_blocks, side, width = feat_hbm.shape
    col_blocks = ext.shape[0]
    halo_blocks = col_blocks - row_blocks
    half = row_blocks // 2
    count = idx_ref.shape[2]
    per = count // side
    slab = rs_wide.shape[1]
    part_width = rs_narrow.shape[2]
    keep_to = nodes_live[0]

    loads = [
        pltpu.make_async_copy(feat_hbm.at[pl.ds(0, half)], ext.at[pl.ds(0, half)], load.at[0]),
        pltpu.make_async_copy(feat_hbm.at[pl.ds(half, half)], ext.at[pl.ds(half, half)], load.at[1]),
        pltpu.make_async_copy(adj_hbm, adj, load.at[2]),
        pltpu.make_async_copy(w_hbm, w_ref, load.at[3]),
        pltpu.make_async_copy(grad_hbm, grad, load.at[4]),
    ]
    for fetch in loads:
        fetch.start()

    def wide_peer(d):
        return (lax.rem(w + d, n_wide), n)

    def narrow_peer(d):
        return (w, lax.rem(n + d, n_narrow))

    def remote(src, dst, s, r, peer):
        return pltpu.make_async_remote_copy(
            src_ref=src, dst_ref=dst, send_sem=s, recv_sem=r, device_id=peer, device_id_type=MESH
        )

    near = neighbours(n_wide, n_narrow)
    peers = [wide_peer(d) for d in range(1, n_wide)] + [
        narrow_peer(d) for d in range(1, n_narrow)
    ]
    barrier = pltpu.get_barrier_semaphore()
    for peer in peers:
        pl.semaphore_signal(barrier, inc=1, device_id=peer, device_id_type=MESH)

    for i, line in enumerate(tables(row_ref, col_ref, pads, live[0], row_blocks, col_blocks)):
        lined[pl.ds(i, 1), :] = line
    tabled = pltpu.make_async_copy(lined, table, load.at[5])
    tabled.start()

    ext[pl.ds(row_blocks, halo_blocks)] = jnp.zeros((halo_blocks, side, width), BF)
    wsum[...] = jnp.zeros_like(wsum)
    bsum[...] = jnp.zeros_like(bsum)
    loads[0].wait()
    span = half * side
    lane = lax.broadcasted_iota(jnp.int32, (count, 128), 1).astype(F32)

    def pack(k):
        row = idx_ref[0, pl.ds(k, 1), :].astype(F32)
        column = jnp.transpose(jnp.broadcast_to(row, (128, count)))
        hot = jnp.concatenate(
            [jnp.where(column == lane + float(at), 1.0, 0.0).astype(BF) for at in range(0, span, 128)],
            axis=1,
        )
        near_rows = ext[pl.ds(0, half)].reshape(span, width)
        packed[k] = jnp.dot(hot, near_rows, preferred_element_type=F32).astype(BF)

    pack(2)
    pl.semaphore_wait(barrier, len(peers))
    for k in (2, 3, 1, 0):
        there, target = near[k]
        if k != 2:
            pack(k)

        @pl.when(there)
        def _():
            halo_copy(packed, landing, send, recv, k, target).start()

    def kept(block, blocks=1):
        at = lax.broadcasted_iota(jnp.int32, (blocks * side, width), 0)
        return at < keep_to - block * side

    loads[1].wait()

    def mask(i, carry):
        ext[i] = jnp.where(kept(i), ext[i].astype(F32), 0.0).astype(BF)
        return carry

    lax.fori_loop(half, row_blocks, mask, 0)
    loads[2].wait()
    tabled.wait()

    def product(k):
        return jnp.dot(adj[table[0, k]], ext[table[1, k]], preferred_element_type=F32)

    unroll = 16

    def leading(t, carry):
        for u in range(unroll):
            k = t * unroll + u
            run[k] = product(k)
        return carry

    lax.fori_loop(0, row_blocks // unroll, leading, 0)
    for k in (1, 0, 2, 3):
        there, target = near[k]

        @pl.when(there)
        def _():
            halo_copy(packed, landing, send, recv, k, target).wait_send()
            halo_copy(packed, landing, send, recv, k ^ 1, target).wait_recv()
            ext[pl.ds(row_blocks + k * per, per)] = landing[k].reshape(per, side, width)

    def following(t, carry):
        for u in range(unroll):
            k = t * unroll + u
            run[k] = run[table[2, k]] + product(k)
        return carry

    lax.fori_loop(row_blocks // unroll, slots // unroll, following, 0)
    loads[3].wait()
    loads[4].wait()

    tall = step * side

    def put(i):
        at = pl.ds(i * step, step)
        return pltpu.make_async_copy(grad.at[at], out_hbm.at[at], out_sem.at[i])

    def put_own(t):
        at = pl.ds(t * unroll, unroll)
        return pltpu.make_async_copy(own_spread.at[at], spread_hbm.at[at], own_sem.at[t])

    def into(i):
        agg = jnp.concatenate([run[table[3, i * step + j]] for j in range(step)], 0).astype(BF)
        return agg, jnp.dot(agg, w_ref[...], preferred_element_type=F32)

    def middle(i, pre):
        at = pl.ds(i * step, step)
        g = grad[at].reshape(tall, width).astype(F32)
        pre = pre + b_ref[...]
        keep = kept(i * step, step)
        sig = 0.5 * jnp.tanh(0.5 * pre) + 0.5
        act = pre * sig
        grad[at] = jnp.where(keep, act, 0.0).astype(BF).reshape(step, side, width)
        put(i).start()
        dpre = jnp.where(keep, g * (sig + act * (1.0 - sig)), 0.0).astype(BF)
        bsum[...] += jnp.sum(dpre.astype(F32).reshape(tall // 8, 8, width), 0)
        return dpre

    def after(i, agg, dpre):
        wsum[...] += lax.dot_general(
            agg, dpre, (((0,), (0,)), ((), ())), preferred_element_type=F32
        )
        ext[pl.ds(i * step, step)] = (
            lax.dot_general(dpre, w_ref[...], (((1,), (1,)), ((), ())), preferred_element_type=F32)
            .astype(BF)
            .reshape(step, side, width)
        )

    group = 8

    def dense(t, carry):
        now = into(t * group)
        for u in range(group):
            i = t * group + u
            later = into(i + 1) if u + 1 < group else None
            dpre = middle(i, now[1])
            after(i, now[0], dpre)
            now = later
        return carry

    lax.fori_loop(0, row_blocks // step // group, dense, 0)
    wg[...] = wsum[...].astype(BF).reshape(n_wide, slab, width)
    bg[...] = jnp.sum(bsum[...], 0, keepdims=True)

    first = []
    for d in range(1, n_wide):
        peer = wide_peer(d)
        c = remote(wg.at[peer[0]], rs_wide.at[d], send_w.at[d], recv_w.at[d], peer)
        c.start()
        first.append(c)
    bias_first = []
    for d in range(1, n_wide):
        c = remote(bg, b_wide.at[d], send_bw.at[d], recv_bw.at[d], wide_peer(d))
        c.start()
        bias_first.append(c)
    run[0] = jnp.zeros(run.shape[1:], run.dtype)

    def spreading(k):
        return lax.dot_general(
            adj[table[4, k]], ext[table[5, k]], (((0,), (0,)), ((), ())), preferred_element_type=F32
        )

    def backward(t, carry):
        held = run[t * unroll]
        for u in range(unroll):
            k = t * unroll + u
            held = held * table[6, k].astype(F32) + spreading(k)
            run[k + 1] = held
        return carry

    early = slots - row_blocks
    lax.fori_loop(0, early // unroll, backward, 0)
    for k in (2, 3, 1, 0):
        there, target = near[k]
        for j in range(per):
            ret[k, pl.ds(j * side, side), :] = run[table[7, k * per + j]].astype(BF)

        @pl.when(there)
        def _():
            halo_copy(ret, incoming, send_r, recv_r, k, target).start()

        @pl.when(jnp.logical_not(there))
        def _():
            incoming[k] = jnp.zeros(incoming.shape[1:], BF)

    total = wg[w].astype(F32)
    for c in first:
        c.wait_recv()
    for d in range(1, n_wide):
        total = total + rs_wide[d].astype(F32)
    bias = bg[...]
    for c in bias_first:
        c.wait_recv()
    for d in range(1, n_wide):
        bias = bias + b_wide[d]
    b_mid[...] = bias
    for j in range(n_narrow):
        part[j] = total[:, j * part_width : (j + 1) * part_width].astype(BF)
    second = []
    for d in range(1, n_narrow):
        peer = narrow_peer(d)
        c = remote(part.at[peer[1]], rs_narrow.at[d], send_n.at[d], recv_n.at[d], peer)
        c.start()
        second.append(c)
    for d in range(1, n_narrow):
        c = remote(b_mid, b_narrow.at[d], send_bn.at[d], recv_bn.at[d], narrow_peer(d))
        c.start()
        bias_first.append(c)
        second.append(c)

    def own(c):
        return run[table[7, halo_blocks + c]] + spreading(early + c)

    def low(t, carry):
        for u in range(unroll):
            c = t * unroll + u
            own_spread[c] = own(c).astype(BF)
        put_own(t).start()
        return carry

    lax.fori_loop(0, half // unroll, low, 0)
    piece = part[n].astype(F32)
    for c in second:
        c.wait_recv()
    for d in range(1, n_narrow):
        piece = piece + rs_narrow[d].astype(F32)
        bias = bias + b_narrow[d]
    bout_ref[...] = bias * scale
    ag_narrow[n] = (piece * scale).astype(BF)
    third = []
    for d in range(1, n_narrow):
        c = remote(ag_narrow.at[n], ag_narrow.at[n], send_gn.at[d], recv_gn.at[d], narrow_peer(d))
        c.start()
        third.append(c)

    def high(t, carry):
        for u in range(unroll):
            c = t * unroll + u
            own_spread[c] = jnp.where(kept(c), own(c), 0.0).astype(BF)
        put_own(t).start()
        return carry

    lax.fori_loop(half // unroll, row_blocks // unroll, high, 0)
    for c in third:
        c.wait_recv()
    fourth = []
    for d in range(1, n_wide):
        c = remote(ag_narrow, ag_wide.at[w], send_gw.at[d], recv_gw.at[d], wide_peer(d))
        c.start()
        fourth.append(c)
    ag_wide[w] = ag_narrow[...]
    for k in range(4):
        there, target = near[k]

        @pl.when(there)
        def _():
            halo_copy(ret, incoming, send_r, recv_r, k, target).wait_send()
            halo_copy(ret, incoming, send_r, recv_r, k ^ 1, target).wait_recv()

    gives = [
        pltpu.make_async_copy(incoming, incoming_hbm, give.at[0]),
        pltpu.make_async_copy(wout_ref, wout_hbm, give.at[1]),
        pltpu.make_async_copy(bout_ref, bout_hbm, give.at[2]),
    ]
    gives[0].start()
    for c in fourth:
        c.wait_recv()
    for i in range(n_wide):
        for j in range(n_narrow):
            wout_ref[pl.ds(i * slab, slab), pl.ds(j * part_width, part_width)] = ag_wide[
                i, j
            ].astype(F32)
    for c in gives[1:]:
        c.start()

    def drain(i, carry):
        put(i).wait()
        return carry

    lax.fori_loop(0, row_blocks // step, drain, 0)
    for t in range(row_blocks // unroll):
        put_own(t).wait()
    for c in gives:
        c.wait()
    for c in first + bias_first + second[: n_narrow - 1] + third + fourth:
        c.wait_send()


def finish_kernel(
    idx_ref,
    spread_hbm,
    incoming_hbm,
    out_in,
    w_in,
    b_in,
    grad_hbm,
    out_hbm,
    w_hbm,
    b_hbm,
    grad,
    incoming,
    out,
    wg,
    bg,
    take,
    give,
    first_take,
):
    chunks, chunk, width = grad.shape
    half = chunks // 2
    heads = [
        pltpu.make_async_copy(incoming_hbm, incoming, first_take.at[0]),
        pltpu.make_async_copy(
            spread_hbm.at[pl.ds(0, half)], grad.at[pl.ds(0, half)], first_take.at[1]
        ),
    ]
    hops = [(out_in.at[i], out.at[i], out_hbm.at[i]) for i in range(out.shape[0])]
    hops += [(spread_hbm.at[i], grad.at[i], grad_hbm.at[i]) for i in range(half, chunks)]
    hops += [(w_in, wg, w_hbm), (b_in, bg, b_hbm)]
    ins = [pltpu.make_async_copy(a, b, take.at[i]) for i, (a, b, _) in enumerate(hops)]
    outs = [pltpu.make_async_copy(b, c, give.at[i]) for i, (_, b, c) in enumerate(hops)]
    for c in heads + ins:
        c.start()
    idx = jnp.concatenate([idx_ref[0, k : k + 1, :] for k in range(incoming.shape[0])], 1)
    for c in heads:
        c.wait()
    merged = incoming[...].reshape(-1, width)
    per = -(-len(hops) // half)
    for i in range(half):
        row = lax.broadcasted_iota(jnp.int32, (chunk, idx.shape[1]), 0) + i * chunk
        hot = jnp.where(row == idx, 1.0, 0.0).astype(BF)
        full = grad[i].astype(F32) + jnp.dot(hot, merged, preferred_element_type=F32)
        grad[i] = full.astype(BF)
        c = pltpu.make_async_copy(grad.at[i], grad_hbm.at[i], give.at[len(hops) + i])
        c.start()
        outs.append(c)
        for j in range(i * per, min(i * per + per, len(hops))):
            ins[j].wait()
            outs[j].start()
    for c in outs:
        c.wait()


def local(
    n_wide,
    n_narrow,
    features,
    adjacency,
    block_rows,
    block_cols,
    block_count,
    node_count,
    halo_index,
    weight,
    bias,
    out_grad,
):
    nodes, width = features.shape
    slots, side, _ = adjacency.shape
    row_blocks = nodes // side
    sides, halo = halo_index.shape[1:]
    halo_blocks = sides * halo // side
    col_blocks = row_blocks + halo_blocks
    vm = pl.BlockSpec(memory_space=pltpu.VMEM)
    sm = pl.BlockSpec(memory_space=pltpu.SMEM)
    hb = pl.BlockSpec(memory_space=ANY)
    dma = pltpu.SemaphoreType.DMA
    shape = jax.ShapeDtypeStruct
    blocked = (row_blocks, side, width)
    lanes = -(-slots // 128) * 128
    slab = width // n_wide
    part_width = width // n_narrow
    scale = 1.0 / math.sqrt(nodes * n_wide * n_narrow)
    step = 2
    chunk = 2 * side
    chunked = (nodes // chunk, chunk, width)
    pieces = 8
    pieced = (pieces, nodes // pieces, width)
    hops = pieces + nodes // chunk // 2 + 2
    out, own_spread, incoming, wout, bout = pl.pallas_call(
        functools.partial(layer_kernel, n_wide, n_narrow, scale, step),
        name="layer",
        out_shape=(
            shape(blocked, BF),
            shape(blocked, BF),
            shape((sides, halo, width), BF),
            shape((width, width), F32),
            shape((1, width), F32),
        ),
        in_specs=[vm, vm, vm, sm, sm, vm, hb, hb, hb, hb],
        out_specs=(hb,) * 5,
        scratch_shapes=[
            pltpu.VMEM(blocked, BF),
            pltpu.VMEM(blocked, BF),
            pltpu.VMEM((sides, halo, width), BF),
            pltpu.VMEM((width, width), F32),
            pltpu.VMEM((1, width), F32),
            pltpu.VMEM((8, lanes), jnp.int32),
            pltpu.VMEM((8, lanes), jnp.int32),
            pltpu.SMEM((8, lanes), jnp.int32),
            pltpu.VMEM((col_blocks, side, width), BF),
            pltpu.VMEM((slots, side, side), BF),
            pltpu.VMEM((width, width), BF),
            pltpu.VMEM((slots, side, width), F32),
            pltpu.VMEM((sides, halo, width), BF),
            pltpu.VMEM((sides, halo, width), BF),
            pltpu.VMEM((sides, halo, width), BF),
            pltpu.VMEM((width, width), F32),
            pltpu.VMEM((n_wide, slab, width), BF),
            pltpu.VMEM((8, width), F32),
            pltpu.VMEM((1, width), F32),
            pltpu.VMEM((n_wide, slab, width), BF),
            pltpu.VMEM((n_narrow, slab, part_width), BF),
            pltpu.VMEM((n_narrow, slab, part_width), BF),
            pltpu.VMEM((n_narrow, slab, part_width), BF),
            pltpu.VMEM((n_wide, n_narrow, slab, part_width), BF),
            pltpu.VMEM((n_wide, 1, width), F32),
            pltpu.VMEM((1, width), F32),
            pltpu.VMEM((n_narrow, 1, width), F32),
            dma((6,)),
            dma((row_blocks // step,)),
            dma((row_blocks,)),
            dma((3,)),
        ]
        + [dma((sides,))] * 4
        + [dma((n_wide,))] * 2
        + [dma((n_narrow,))] * 4
        + [dma((n_wide,))] * 4
        + [dma((n_narrow,))] * 2,
        compiler_params=pltpu.CompilerParams(
            collective_id=0, has_side_effects=True, vmem_limit_bytes=VMEM_LIMIT
        ),
    )(
        halo_index,
        block_rows,
        block_cols,
        block_count,
        node_count,
        bias.reshape(1, width),
        features.reshape(blocked),
        adjacency,
        out_grad.reshape(blocked),
        weight,
    )
    input_grad, out, wout, bout = pl.pallas_call(
        finish_kernel,
        name="finish",
        out_shape=(
            shape(chunked, BF),
            shape(pieced, BF),
            shape((width, width), F32),
            shape((1, width), F32),
        ),
        in_specs=[vm, hb, hb, hb, hb, hb],
        out_specs=(hb, hb, hb, hb),
        scratch_shapes=[
            pltpu.VMEM(chunked, BF),
            pltpu.VMEM((sides, halo, width), BF),
            pltpu.VMEM(pieced, BF),
            pltpu.VMEM((width, width), F32),
            pltpu.VMEM((1, width), F32),
            dma((hops,)),
            dma((hops + nodes // chunk // 2,)),
            dma((2,)),
        ],
        compiler_params=pltpu.CompilerParams(vmem_limit_bytes=FINISH_LIMIT),
    )(halo_index, own_spread.reshape(chunked), incoming, out.reshape(pieced), wout, bout)
    return out.reshape(nodes, width), input_grad.reshape(nodes, width), wout, bout.reshape(width)


def solution(mesh):
    both = ("wide", "narrow")
    placed = (
        P(both, None),
        P(both, None, None),
        P(both, None),
        P(both, None),
        P(both),
        P(both),
        P(both, None, None),
        P(),
        P(),
        P(both, None),
    )
    return jax.shard_map(
        functools.partial(local, mesh.shape["wide"], mesh.shape["narrow"]),
        mesh=mesh,
        in_specs=placed,
        out_specs=(P(both, None), P(both, None), P(), P()),
        check_vma=False,
    )
```

time: 73.3 us -> 65.8 us (0.90)
  Pallas kernels: 71.5 us -> 63.4 us
    pallas_call x4 -> x2, Pallas kernels: 71.5 us -> 63.4 us  [the longest x1 55.1 us: local(): pl.pallas_call(functools.partial(layer_kernel, n_wide, n_narrow, scale, s...]
where the time goes in v1:
time: 65.8 us; the launch traced here: 65.5 us
  Pallas kernels  63.4 us (96%)
  between operations  2.09 us (3%)
    pallas_call x1, Pallas kernels, local(): pl.pallas_call(functools.partial(layer_kernel, n_wide, n_narrow, scale, s...  55.1 us
    pallas_call x1, Pallas kernels, local(): pl.pallas_call(finish_kernel, name='finish', out_shape=(shape(chunked, BF...  8.23 us

profile of v1, /device:TPU:0, one launch (start us, length us, event | category | flops | bytes accessed | tf_op | source)
XLA Modules:
  0.0 65.5 jit_solution(6030680332377559413)
XLA Ops:
  1.9 55.1 %layer.1 = (bf16[32,128,512]{2,1,0:T(8,128)(2,1)}, bf16[32,128,512]{2,1,0:T(8,128)(2,1)}, bf16[4,256,512]{2,1,0:T(8,128)(2,1)}, f32[512,512]{1,0:T(8,128)}, f32[1,512]{1,0:T(1,128)}) custom-call(s32[1,4,256]{2,1,0:T(4,128)} %idx_ref.3, s32[1,96]{1,0:T(1,128)} %row_ref.1, s32[1,96]{1,0:T(1,128)} %col_ref.1, s32[1]{0:T(128)S(6)} %copy.14.live, ...), custom_call_target="tpu_custom_call" | custom-call | tf_op jit(solution)/shard_map/layer/pallas_call | solution.py:574
  57.1 8.2 %finish.1 = (bf16[16,256,512]{2,1,0:T(8,128)(2,1)}, bf16[8,512,512]{2,1,0:T(8,128)(2,1)}, f32[512,512]{1,0:T(8,128)}, f32[1,512]{1,0:T(1,128)}) custom-call(s32[1,4,256]{2,1,0:T(4,128)} %idx_ref.3, bf16[16,256,512]{2,1,0:T(8,128)(2,1)} %bitcast.11, bf16[4,256,512]{2,1,0:T(8,128)(2,1)} %get-tuple-element.14.incoming_hbm, bf16[8,512,512]{2,1,0:T(8,128)(2,1)} %bitcast.10, ...), custom_call_target="tpu_custom_call" | custom-call | tf_op jit(solution)/shard_map/finish/pallas_call | solution.py:639

commit v2 on v1

--- a/solution.py
+++ b/solution.py
@@ -10,8 +10,8 @@
 
 MESH = pl.DeviceIdType.MESH
 ANY = pl.ANY
-VMEM_LIMIT = 60 * 1024 * 1024
-FINISH_LIMIT = 60 * 1024 * 1024
+VMEM_LIMIT = 48 * 1024 * 1024
+FINISH_LIMIT = 16 * 1024 * 1024
 BF = jnp.bfloat16
 F32 = jnp.float32
 
@@ -110,15 +110,10 @@
     adj_hbm,
     grad_hbm,
     w_hbm,
-    out_hbm,
-    spread_hbm,
-    incoming_hbm,
-    wout_hbm,
-    bout_hbm,
     grad,
     own_spread,
     incoming,
-    wout_ref,
+    ag_wide,
     bout_ref,
     pads,
     lined,
@@ -138,14 +133,10 @@
     rs_narrow,
     part,
     ag_narrow,
-    ag_wide,
     b_wide,
     b_mid,
     b_narrow,
     load,
-    out_sem,
-    own_sem,
-    give,
     send,
     recv,
     send_r,
@@ -285,14 +276,6 @@
 
     tall = step * side
 
-    def put(i):
-        at = pl.ds(i * step, step)
-        return pltpu.make_async_copy(grad.at[at], out_hbm.at[at], out_sem.at[i])
-
-    def put_own(t):
-        at = pl.ds(t * unroll, unroll)
-        return pltpu.make_async_copy(own_spread.at[at], spread_hbm.at[at], own_sem.at[t])
-
     def into(i):
         agg = jnp.concatenate([run[table[3, i * step + j]] for j in range(step)], 0).astype(BF)
         return agg, jnp.dot(agg, w_ref[...], preferred_element_type=F32)
@@ -305,7 +288,6 @@
         sig = 0.5 * jnp.tanh(0.5 * pre) + 0.5
         act = pre * sig
         grad[at] = jnp.where(keep, act, 0.0).astype(BF).reshape(step, side, width)
-        put(i).start()
         dpre = jnp.where(keep, g * (sig + act * (1.0 - sig)), 0.0).astype(BF)
         bsum[...] += jnp.sum(dpre.astype(F32).reshape(tall // 8, 8, width), 0)
         return dpre
@@ -314,11 +296,7 @@
         wsum[...] += lax.dot_general(
             agg, dpre, (((0,), (0,)), ((), ())), preferred_element_type=F32
         )
-        ext[pl.ds(i * step, step)] = (
-            lax.dot_general(dpre, w_ref[...], (((1,), (1,)), ((), ())), preferred_element_type=F32)
-            .astype(BF)
-            .reshape(step, side, width)
-        )
+        ext[pl.ds(i * step, step)] = dpre.reshape(step, side, width)
 
     group = 8
 
@@ -348,6 +326,23 @@
         c.start()
         bias_first.append(c)
     run[0] = jnp.zeros(run.shape[1:], run.dtype)
+    deep = 8
+
+    def backed(t, carry):
+        at = pl.ds(t * deep, deep)
+        ext[at] = (
+            lax.dot_general(
+                ext[at].reshape(deep * side, width),
+                w_ref[...],
+                (((1,), (1,)), ((), ())),
+                preferred_element_type=F32,
+            )
+            .astype(BF)
+            .reshape(deep, side, width)
+        )
+        return carry
+
+    lax.fori_loop(0, row_blocks // deep, backed, 0)
 
     def spreading(k):
         return lax.dot_general(
@@ -364,19 +359,6 @@
 
     early = slots - row_blocks
     lax.fori_loop(0, early // unroll, backward, 0)
-    for k in (2, 3, 1, 0):
-        there, target = near[k]
-        for j in range(per):
-            ret[k, pl.ds(j * side, side), :] = run[table[7, k * per + j]].astype(BF)
-
-        @pl.when(there)
-        def _():
-            halo_copy(ret, incoming, send_r, recv_r, k, target).start()
-
-        @pl.when(jnp.logical_not(there))
-        def _():
-            incoming[k] = jnp.zeros(incoming.shape[1:], BF)
-
     total = wg[w].astype(F32)
     for c in first:
         c.wait_recv()
@@ -402,6 +384,33 @@
         bias_first.append(c)
         second.append(c)
 
+    def returned(k, j):
+        at = pl.ds(j * side, side)
+        return pltpu.make_async_remote_copy(
+            src_ref=ret.at[k, at],
+            dst_ref=incoming.at[k ^ 1, at],
+            send_sem=send_r.at[k, j],
+            recv_sem=recv_r.at[k ^ 1, j],
+            device_id=near[k][1],
+            device_id_type=MESH,
+        )
+
+    def give_back(k, j):
+        ret[k, pl.ds(j * side, side), :] = run[table[7, k * per + j]].astype(BF)
+
+        @pl.when(near[k][0])
+        def _():
+            returned(k, j).start()
+
+        @pl.when(jnp.logical_not(near[k][0]))
+        def _():
+            incoming[k, pl.ds(j * side, side), :] = jnp.zeros((side, width), BF)
+
+    early_return = [(k, j) for k in (2, 3) for j in range(per // 2)]
+    early_return += [(k, j) for k in (1, 0) for j in range(per)]
+    for k, j in early_return:
+        give_back(k, j)
+
     def own(c):
         return run[table[7, halo_blocks + c]] + spreading(early + c)
 
@@ -409,7 +418,6 @@
         for u in range(unroll):
             c = t * unroll + u
             own_spread[c] = own(c).astype(BF)
-        put_own(t).start()
         return carry
 
     lax.fori_loop(0, half // unroll, low, 0)
@@ -426,12 +434,14 @@
         c = remote(ag_narrow.at[n], ag_narrow.at[n], send_gn.at[d], recv_gn.at[d], narrow_peer(d))
         c.start()
         third.append(c)
+    for k in (2, 3):
+        for j in range(per // 2, per):
+            give_back(k, j)
 
     def high(t, carry):
         for u in range(unroll):
             c = t * unroll + u
             own_spread[c] = jnp.where(kept(c), own(c), 0.0).astype(BF)
-        put_own(t).start()
         return carry
 
     lax.fori_loop(half // unroll, row_blocks // unroll, high, 0)
@@ -448,90 +458,70 @@
 
         @pl.when(there)
         def _():
-            halo_copy(ret, incoming, send_r, recv_r, k, target).wait_send()
-            halo_copy(ret, incoming, send_r, recv_r, k ^ 1, target).wait_recv()
-
-    gives = [
-        pltpu.make_async_copy(incoming, incoming_hbm, give.at[0]),
-        pltpu.make_async_copy(wout_ref, wout_hbm, give.at[1]),
-        pltpu.make_async_copy(bout_ref, bout_hbm, give.at[2]),
-    ]
-    gives[0].start()
+            for j in range(per):
+                returned(k, j).wait_send()
+                returned(k ^ 1, j).wait_recv()
+
     for c in fourth:
         c.wait_recv()
-    for i in range(n_wide):
-        for j in range(n_narrow):
-            wout_ref[pl.ds(i * slab, slab), pl.ds(j * part_width, part_width)] = ag_wide[
-                i, j
-            ].astype(F32)
-    for c in gives[1:]:
-        c.start()
-
-    def drain(i, carry):
-        put(i).wait()
-        return carry
-
-    lax.fori_loop(0, row_blocks // step, drain, 0)
-    for t in range(row_blocks // unroll):
-        put_own(t).wait()
-    for c in gives:
-        c.wait()
     for c in first + bias_first + second[: n_narrow - 1] + third + fourth:
         c.wait_send()
 
 
 def finish_kernel(
     idx_ref,
-    spread_hbm,
-    incoming_hbm,
-    out_in,
-    w_in,
-    b_in,
+    spread_ref,
+    incoming,
+    out_ref,
+    ag_wide,
+    b_ref,
     grad_hbm,
     out_hbm,
     w_hbm,
     b_hbm,
     grad,
-    incoming,
-    out,
     wg,
-    bg,
-    take,
     give,
-    first_take,
+    part_give,
 ):
-    chunks, chunk, width = grad.shape
-    half = chunks // 2
-    heads = [
-        pltpu.make_async_copy(incoming_hbm, incoming, first_take.at[0]),
+    half, chunk, width = grad.shape
+    n_wide, n_narrow, slab, part_width = ag_wide.shape
+    moves = [
+        pltpu.make_async_copy(out_ref, out_hbm, give.at[0]),
         pltpu.make_async_copy(
-            spread_hbm.at[pl.ds(0, half)], grad.at[pl.ds(0, half)], first_take.at[1]
+            spread_ref.at[pl.ds(half, half)], grad_hbm.at[pl.ds(half, half)], give.at[1]
         ),
+        pltpu.make_async_copy(b_ref, b_hbm, give.at[2]),
     ]
-    hops = [(out_in.at[i], out.at[i], out_hbm.at[i]) for i in range(out.shape[0])]
-    hops += [(spread_hbm.at[i], grad.at[i], grad_hbm.at[i]) for i in range(half, chunks)]
-    hops += [(w_in, wg, w_hbm), (b_in, bg, b_hbm)]
-    ins = [pltpu.make_async_copy(a, b, take.at[i]) for i, (a, b, _) in enumerate(hops)]
-    outs = [pltpu.make_async_copy(b, c, give.at[i]) for i, (_, b, c) in enumerate(hops)]
-    for c in heads + ins:
+    for c in moves:
         c.start()
+    for i in range(n_wide):
+        for j in range(n_narrow):
+            wg[pl.ds(i * slab, slab), pl.ds(j * part_width, part_width)] = ag_wide[i, j].astype(F32)
+    moves.append(pltpu.make_async_copy(wg, w_hbm, give.at[3]))
+    moves[3].start()
+    merged = incoming[...].reshape(-1, width)
     idx = jnp.concatenate([idx_ref[0, k : k + 1, :] for k in range(incoming.shape[0])], 1)
-    for c in heads:
-        c.wait()
-    merged = incoming[...].reshape(-1, width)
-    per = -(-len(hops) // half)
-    for i in range(half):
+
+    def leave(i):
+        return pltpu.make_async_copy(grad.at[i], grad_hbm.at[i], part_give.at[i])
+
+    def scatter(i, carry):
         row = lax.broadcasted_iota(jnp.int32, (chunk, idx.shape[1]), 0) + i * chunk
         hot = jnp.where(row == idx, 1.0, 0.0).astype(BF)
-        full = grad[i].astype(F32) + jnp.dot(hot, merged, preferred_element_type=F32)
+        full = spread_ref[i].astype(F32) + jnp.dot(hot, merged, preferred_element_type=F32)
         grad[i] = full.astype(BF)
-        c = pltpu.make_async_copy(grad.at[i], grad_hbm.at[i], give.at[len(hops) + i])
-        c.start()
-        outs.append(c)
-        for j in range(i * per, min(i * per + per, len(hops))):
-            ins[j].wait()
-            outs[j].start()
-    for c in outs:
+        leave(i).start()
+        return carry
+
+    lax.fori_loop(0, half, scatter, 0)
+
+    def drain(i, carry):
+        leave(i).wait()
+        return carry
+
+    lax.fori_loop(0, half, drain, 0)
+    for c in moves:
         c.wait()
 
 
@@ -568,27 +558,20 @@
     step = 2
     chunk = 2 * side
     chunked = (nodes // chunk, chunk, width)
-    pieces = 8
-    pieced = (pieces, nodes // pieces, width)
-    hops = pieces + nodes // chunk // 2 + 2
-    out, own_spread, incoming, wout, bout = pl.pallas_call(
+    half = nodes // chunk // 2
+    out, own_spread, incoming, gathered, bout = pl.pallas_call(
         functools.partial(layer_kernel, n_wide, n_narrow, scale, step),
         name="layer",
         out_shape=(
-            shape(blocked, BF),
-            shape(blocked, BF),
-            shape((sides, halo, width), BF),
-            shape((width, width), F32),
-            shape((1, width), F32),
-        ),
-        in_specs=[vm, vm, vm, sm, sm, vm, hb, hb, hb, hb],
-        out_specs=(hb,) * 5,
-        scratch_shapes=[
             pltpu.VMEM(blocked, BF),
             pltpu.VMEM(blocked, BF),
             pltpu.VMEM((sides, halo, width), BF),
-            pltpu.VMEM((width, width), F32),
+            pltpu.VMEM((n_wide, n_narrow, slab, part_width), BF),
             pltpu.VMEM((1, width), F32),
+        ),
+        in_specs=[vm, vm, vm, sm, sm, vm, hb, hb, hb, hb],
+        out_specs=(vm,) * 5,
+        scratch_shapes=[
             pltpu.VMEM((8, lanes), jnp.int32),
             pltpu.VMEM((8, lanes), jnp.int32),
             pltpu.SMEM((8, lanes), jnp.int32),
@@ -607,16 +590,13 @@
             pltpu.VMEM((n_narrow, slab, part_width), BF),
             pltpu.VMEM((n_narrow, slab, part_width), BF),
             pltpu.VMEM((n_narrow, slab, part_width), BF),
-            pltpu.VMEM((n_wide, n_narrow, slab, part_width), BF),
             pltpu.VMEM((n_wide, 1, width), F32),
             pltpu.VMEM((1, width), F32),
             pltpu.VMEM((n_narrow, 1, width), F32),
             dma((6,)),
-            dma((row_blocks // step,)),
-            dma((row_blocks,)),
-            dma((3,)),
         ]
-        + [dma((sides,))] * 4
+        + [dma((sides,))] * 2
+        + [dma((sides, halo // side))] * 2
         + [dma((n_wide,))] * 2
         + [dma((n_narrow,))] * 4
         + [dma((n_wide,))] * 4
@@ -641,24 +621,20 @@
         name="finish",
         out_shape=(
             shape(chunked, BF),
-            shape(pieced, BF),
+            shape(blocked, BF),
             shape((width, width), F32),
             shape((1, width), F32),
         ),
-        in_specs=[vm, hb, hb, hb, hb, hb],
+        in_specs=[vm] * 6,
         out_specs=(hb, hb, hb, hb),
         scratch_shapes=[
-            pltpu.VMEM(chunked, BF),
-            pltpu.VMEM((sides, halo, width), BF),
-            pltpu.VMEM(pieced, BF),
+            pltpu.VMEM((half, chunk, width), BF),
             pltpu.VMEM((width, width), F32),
-            pltpu.VMEM((1, width), F32),
-            dma((hops,)),
-            dma((hops + nodes // chunk // 2,)),
-            dma((2,)),
+            dma((4,)),
+            dma((half,)),
         ],
         compiler_params=pltpu.CompilerParams(vmem_limit_bytes=FINISH_LIMIT),
-    )(halo_index, own_spread.reshape(chunked), incoming, out.reshape(pieced), wout, bout)
+    )(halo_index, own_spread.reshape(chunked), incoming, out, gathered, bout)
     return out.reshape(nodes, width), input_grad.reshape(nodes, width), wout, bout.reshape(width)
 
 

time: 65.8 us -> 57.6 us (0.88)
  Pallas kernels: 63.4 us -> 55.4 us
    pallas_call x1, Pallas kernels: 55.1 us -> 50.9 us  [local(): pl.pallas_call(functools.partial(layer_kernel, n_wide, n_narrow, scale, s...]
    pallas_call x1, Pallas kernels: 8.23 us -> 4.54 us  [local(): pl.pallas_call(finish_kernel, name='finish', out_shape=(shape(chunked, BF...]
where the time goes in v2:
time: 57.6 us; the launch traced here: 57.4 us
  Pallas kernels  55.4 us (96%)
  between operations  1.95 us (3%)
    pallas_call x1, Pallas kernels, local(): pl.pallas_call(functools.partial(layer_kernel, n_wide, n_narrow, scale, s...  50.9 us
    pallas_call x1, Pallas kernels, local(): pl.pallas_call(finish_kernel, name='finish', out_shape=(shape(chunked, BF...  4.54 us

profile of v2, /device:TPU:0, one launch (start us, length us, event | category | flops | bytes accessed | tf_op | source)
XLA Modules:
  0.0 57.4 jit_solution(16384871406233317135)
XLA Ops:
  1.9 0.0 copy-start
  1.9 50.9 %layer.1 = (bf16[32,128,512]{2,1,0:T(8,128)(2,1)S(1)}, bf16[32,128,512]{2,1,0:T(8,128)(2,1)S(1)}, bf16[4,256,512]{2,1,0:T(8,128)(2,1)S(1)}, bf16[8,4,64,128]{3,2,1,0:T(8,128)(2,1)S(1)}, f32[1,512]{1,0:T(1,128)S(1)}) custom-call(s32[1,4,256]{2,1,0:T(4,128)} %idx_ref.3, s32[1,96]{1,0:T(1,128)} %row_ref.1, s32[1,96]{1,0:T(1,128)} %col_ref.1, s32[1]{0:T(128)S(6)} %copy.14.live, ...), custom_call_target="tpu_custom_call" | custom-call | tf_op jit(solution)/shard_map/layer/pallas_call | solution.py:562
  52.8 0.0 copy-done
  52.9 4.5 %finish.1 = (bf16[16,256,512]{2,1,0:T(8,128)(2,1)}, bf16[32,128,512]{2,1,0:T(8,128)(2,1)}, f32[512,512]{1,0:T(8,128)}, f32[1,512]{1,0:T(1,128)}) custom-call(s32[1,4,256]{2,1,0:T(4,128)S(1)} %copy-done, bf16[16,256,512]{2,1,0:T(8,128)(2,1)S(1)} %bitcast.7, bf16[4,256,512]{2,1,0:T(8,128)(2,1)S(1)} %get-tuple-element.14.incoming, ...), custom_call_target="tpu_custom_call" | custom-call | tf_op jit(solution)/shard_map/finish/pallas_call | solution.py:619
Async XLA Ops:
  1.9 50.9 %copy-start = (s32[1,4,256]{2,1,0:T(4,128)S(1)}, s32[1,4,256]{2,1,0:T(4,128)}, u32[]{:S(2)}) copy-start(s32[1,4,256]{2,1,0:T(4,128)} %idx_ref.3) | copy-start | bytes 12292

commit v3 on v2

--- a/solution.py
+++ b/solution.py
@@ -163,8 +163,8 @@
     half = row_blocks // 2
     count = idx_ref.shape[2]
     per = count // side
-    slab = rs_wide.shape[1]
-    part_width = rs_narrow.shape[2]
+    slab, across = rs_wide.shape[2:]
+    part_width = rs_narrow.shape[3]
     keep_to = nodes_live[0]
 
     loads = [
@@ -276,55 +276,121 @@
 
     tall = step * side
 
-    def into(i):
-        agg = jnp.concatenate([run[table[3, i * step + j]] for j in range(step)], 0).astype(BF)
-        return agg, jnp.dot(agg, w_ref[...], preferred_element_type=F32)
-
-    def middle(i, pre):
+    def into(i, h):
         at = pl.ds(i * step, step)
-        g = grad[at].reshape(tall, width).astype(F32)
-        pre = pre + b_ref[...]
-        keep = kept(i * step, step)
+        if h == 0:
+            agg = jnp.concatenate([run[table[3, i * step + j]] for j in range(step)], 0).astype(BF)
+            own_spread[at] = agg.reshape(step, side, width)
+        else:
+            agg = own_spread[at].reshape(tall, width)
+        return agg, jnp.dot(agg, w_ref[:, cut(h)], preferred_element_type=F32)
+
+    def cut(h):
+        return slice(h * across, (h + 1) * across)
+
+    def middle(i, pre, h):
+        at = pl.ds(i * step, step)
+        g = grad[at, :, cut(h)].reshape(tall, across).astype(F32)
+        pre = pre + b_ref[:, cut(h)]
+        at_row = lax.broadcasted_iota(jnp.int32, (tall, across), 0)
+        keep = at_row < keep_to - i * tall
         sig = 0.5 * jnp.tanh(0.5 * pre) + 0.5
         act = pre * sig
-        grad[at] = jnp.where(keep, act, 0.0).astype(BF).reshape(step, side, width)
+        grad[at, :, cut(h)] = jnp.where(keep, act, 0.0).astype(BF).reshape(step, side, across)
         dpre = jnp.where(keep, g * (sig + act * (1.0 - sig)), 0.0).astype(BF)
-        bsum[...] += jnp.sum(dpre.astype(F32).reshape(tall // 8, 8, width), 0)
+        bsum[:, cut(h)] += jnp.sum(dpre.astype(F32).reshape(tall // 8, 8, across), 0)
         return dpre
 
-    def after(i, agg, dpre):
-        wsum[...] += lax.dot_general(
+    def after(i, agg, dpre, h):
+        wsum[h] += lax.dot_general(
             agg, dpre, (((0,), (0,)), ((), ())), preferred_element_type=F32
         )
-        ext[pl.ds(i * step, step)] = dpre.reshape(step, side, width)
-
-    group = 8
-
-    def dense(t, carry):
-        now = into(t * group)
-        for u in range(group):
-            i = t * group + u
-            later = into(i + 1) if u + 1 < group else None
-            dpre = middle(i, now[1])
-            after(i, now[0], dpre)
-            now = later
-        return carry
-
-    lax.fori_loop(0, row_blocks // step // group, dense, 0)
-    wg[...] = wsum[...].astype(BF).reshape(n_wide, slab, width)
+        ext[pl.ds(i * step, step), :, cut(h)] = dpre.reshape(step, side, across)
+
+    group = row_blocks // step // 2
+
+    def dense(h):
+        def body(t, carry):
+            now = into(t * group, h)
+            for u in range(group):
+                i = t * group + u
+                later = into(i + 1, h) if u + 1 < group else None
+                dpre = middle(i, now[1], h)
+                after(i, now[0], dpre, h)
+                now = later
+            return carry
+
+        lax.fori_loop(0, row_blocks // step // group, body, 0)
+
+    def scatter_wide(h):
+        wg[h] = wsum[h].astype(BF).reshape(n_wide, slab, across)
+        copies = []
+        for d in range(1, n_wide):
+            peer = wide_peer(d)
+            c = remote(
+                wg.at[h, peer[0]], rs_wide.at[h, d], send_w.at[h, d], recv_w.at[h, d], peer
+            )
+            c.start()
+            copies.append(c)
+        return copies
+
+    def scatter_narrow(h, arrived):
+        total = wg[h, w].astype(F32)
+        for c in arrived:
+            c.wait_recv()
+        for d in range(1, n_wide):
+            total = total + rs_wide[h, d].astype(F32)
+        for j in range(n_narrow):
+            part[h, j] = total[:, j * part_width : (j + 1) * part_width].astype(BF)
+        copies = []
+        for d in range(1, n_narrow):
+            peer = narrow_peer(d)
+            c = remote(
+                part.at[h, peer[1]], rs_narrow.at[h, d], send_n.at[h, d], recv_n.at[h, d], peer
+            )
+            c.start()
+            copies.append(c)
+        return copies
+
+    def share_narrow(h, arrived):
+        piece = part[h, n].astype(F32)
+        for c in arrived:
+            c.wait_recv()
+        for d in range(1, n_narrow):
+            piece = piece + rs_narrow[h, d].astype(F32)
+        ag_narrow[h, n] = (piece * scale).astype(BF)
+        copies = []
+        for d in range(1, n_narrow):
+            mine = ag_narrow.at[h, n]
+            c = remote(mine, mine, send_gn.at[h, d], recv_gn.at[h, d], narrow_peer(d))
+            c.start()
+            copies.append(c)
+        return copies
+
+    def share_wide(h, arrived):
+        for c in arrived:
+            c.wait_recv()
+        copies = []
+        for d in range(1, n_wide):
+            c = remote(
+                ag_narrow.at[h], ag_wide.at[h, w], send_gw.at[h, d], recv_gw.at[h, d], wide_peer(d)
+            )
+            c.start()
+            copies.append(c)
+        ag_wide[h, w] = ag_narrow[h]
+        return copies
+
+    dense(0)
+    first = [scatter_wide(0)]
+    dense(1)
+    first.append(scatter_wide(1))
     bg[...] = jnp.sum(bsum[...], 0, keepdims=True)
-
-    first = []
-    for d in range(1, n_wide):
-        peer = wide_peer(d)
-        c = remote(wg.at[peer[0]], rs_wide.at[d], send_w.at[d], recv_w.at[d], peer)
-        c.start()
-        first.append(c)
     bias_first = []
     for d in range(1, n_wide):
         c = remote(bg, b_wide.at[d], send_bw.at[d], recv_bw.at[d], wide_peer(d))
         c.start()
         bias_first.append(c)
+    second = [scatter_narrow(0, first[0])]
     run[0] = jnp.zeros(run.shape[1:], run.dtype)
     deep = 8
 
@@ -343,6 +409,7 @@
         return carry
 
     lax.fori_loop(0, row_blocks // deep, backed, 0)
+    third = [share_narrow(0, second[0])]
 
     def spreading(k):
         return lax.dot_general(
@@ -359,30 +426,19 @@
 
     early = slots - row_blocks
     lax.fori_loop(0, early // unroll, backward, 0)
-    total = wg[w].astype(F32)
-    for c in first:
-        c.wait_recv()
-    for d in range(1, n_wide):
-        total = total + rs_wide[d].astype(F32)
+    fourth = [share_wide(0, third[0])]
+    second.append(scatter_narrow(1, first[1]))
     bias = bg[...]
     for c in bias_first:
         c.wait_recv()
     for d in range(1, n_wide):
         bias = bias + b_wide[d]
     b_mid[...] = bias
-    for j in range(n_narrow):
-        part[j] = total[:, j * part_width : (j + 1) * part_width].astype(BF)
-    second = []
-    for d in range(1, n_narrow):
-        peer = narrow_peer(d)
-        c = remote(part.at[peer[1]], rs_narrow.at[d], send_n.at[d], recv_n.at[d], peer)
-        c.start()
-        second.append(c)
+    bias_second = []
     for d in range(1, n_narrow):
         c = remote(b_mid, b_narrow.at[d], send_bn.at[d], recv_bn.at[d], narrow_peer(d))
         c.start()
-        bias_first.append(c)
-        second.append(c)
+        bias_second.append(c)
 
     def returned(k, j):
         at = pl.ds(j * side, side)
@@ -421,19 +477,12 @@
         return carry
 
     lax.fori_loop(0, half // unroll, low, 0)
-    piece = part[n].astype(F32)
-    for c in second:
+    third.append(share_narrow(1, second[1]))
+    for c in bias_second:
         c.wait_recv()
     for d in range(1, n_narrow):
-        piece = piece + rs_narrow[d].astype(F32)
         bias = bias + b_narrow[d]
     bout_ref[...] = bias * scale
-    ag_narrow[n] = (piece * scale).astype(BF)
-    third = []
-    for d in range(1, n_narrow):
-        c = remote(ag_narrow.at[n], ag_narrow.at[n], send_gn.at[d], recv_gn.at[d], narrow_peer(d))
-        c.start()
-        third.append(c)
     for k in (2, 3):
         for j in range(per // 2, per):
             give_back(k, j)
@@ -445,14 +494,7 @@
         return carry
 
     lax.fori_loop(half // unroll, row_blocks // unroll, high, 0)
-    for c in third:
-        c.wait_recv()
-    fourth = []
-    for d in range(1, n_wide):
-        c = remote(ag_narrow, ag_wide.at[w], send_gw.at[d], recv_gw.at[d], wide_peer(d))
-        c.start()
-        fourth.append(c)
-    ag_wide[w] = ag_narrow[...]
+    fourth.append(share_wide(1, third[1]))
     for k in range(4):
         there, target = near[k]
 
@@ -462,10 +504,12 @@
                 returned(k, j).wait_send()
                 returned(k ^ 1, j).wait_recv()
 
-    for c in fourth:
-        c.wait_recv()
-    for c in first + bias_first + second[: n_narrow - 1] + third + fourth:
-        c.wait_send()
+    for copies in fourth:
+        for c in copies:
+            c.wait_recv()
+    for copies in first + second + third + fourth + [bias_first, bias_second]:
+        for c in copies:
+            c.wait_send()
 
 
 def finish_kernel(
@@ -485,7 +529,7 @@
     part_give,
 ):
     half, chunk, width = grad.shape
-    n_wide, n_narrow, slab, part_width = ag_wide.shape
+    parts, n_wide, n_narrow, slab, part_width = ag_wide.shape
     moves = [
         pltpu.make_async_copy(out_ref, out_hbm, give.at[0]),
         pltpu.make_async_copy(
@@ -496,8 +540,8 @@
     for c in moves:
         c.start()
     for i in range(n_wide):
-        for j in range(n_narrow):
-            wg[pl.ds(i * slab, slab), pl.ds(j * part_width, part_width)] = ag_wide[i, j].astype(F32)
+        line = [ag_wide[h, i, j] for h in range(parts) for j in range(n_narrow)]
+        wg[pl.ds(i * slab, slab), :] = jnp.concatenate(line, 1).astype(F32)
     moves.append(pltpu.make_async_copy(wg, w_hbm, give.at[3]))
     moves[3].start()
     merged = incoming[...].reshape(-1, width)
@@ -553,9 +597,11 @@
     blocked = (row_blocks, side, width)
     lanes = -(-slots // 128) * 128
     slab = width // n_wide
-    part_width = width // n_narrow
+    parts = 2
+    across = width // parts
+    part_width = across // n_narrow
     scale = 1.0 / math.sqrt(nodes * n_wide * n_narrow)
-    step = 2
+    step = 4
     chunk = 2 * side
     chunked = (nodes // chunk, chunk, width)
     half = nodes // chunk // 2
@@ -566,7 +612,7 @@
             pltpu.VMEM(blocked, BF),
             pltpu.VMEM(blocked, BF),
             pltpu.VMEM((sides, halo, width), BF),
-            pltpu.VMEM((n_wide, n_narrow, slab, part_width), BF),
+            pltpu.VMEM((parts, n_wide, n_narrow, slab, part_width), BF),
             pltpu.VMEM((1, width), F32),
         ),
         in_specs=[vm, vm, vm, sm, sm, vm, hb, hb, hb, hb],
@@ -582,14 +628,14 @@
             pltpu.VMEM((sides, halo, width), BF),
             pltpu.VMEM((sides, halo, width), BF),
             pltpu.VMEM((sides, halo, width), BF),
-            pltpu.VMEM((width, width), F32),
-            pltpu.VMEM((n_wide, slab, width), BF),
+            pltpu.VMEM((parts, width, across), F32),
+            pltpu.VMEM((parts, n_wide, slab, across), BF),
             pltpu.VMEM((8, width), F32),
             pltpu.VMEM((1, width), F32),
-            pltpu.VMEM((n_wide, slab, width), BF),
-            pltpu.VMEM((n_narrow, slab, part_width), BF),
-            pltpu.VMEM((n_narrow, slab, part_width), BF),
-            pltpu.VMEM((n_narrow, slab, part_width), BF),
+            pltpu.VMEM((parts, n_wide, slab, across), BF),
+            pltpu.VMEM((parts, n_narrow, slab, part_width), BF),
+            pltpu.VMEM((parts, n_narrow, slab, part_width), BF),
+            pltpu.VMEM((parts, n_narrow, slab, part_width), BF),
             pltpu.VMEM((n_wide, 1, width), F32),
             pltpu.VMEM((1, width), F32),
             pltpu.VMEM((n_narrow, 1, width), F32),
@@ -597,9 +643,10 @@
         ]
         + [dma((sides,))] * 2
         + [dma((sides, halo // side))] * 2
+        + [dma((parts, n_wide))] * 2
+        + [dma((parts, n_narrow))] * 4
+        + [dma((parts, n_wide))] * 2
         + [dma((n_wide,))] * 2
-        + [dma((n_narrow,))] * 4
-        + [dma((n_wide,))] * 4
         + [dma((n_narrow,))] * 2,
         compiler_params=pltpu.CompilerParams(
             collective_id=0, has_side_effects=True, vmem_limit_bytes=VMEM_LIMIT

time: 57.6 us -> 59.7 us (1.036)
  Pallas kernels: 55.4 us -> 57.6 us
    pallas_call x1, Pallas kernels: 50.9 us -> 52.9 us  [local(): pl.pallas_call(functools.partial(layer_kernel, n_wide, n_narrow, scale, s...]
where the time goes in v3:
time: 59.7 us; the launch traced here: 59.5 us
  Pallas kernels  57.6 us (96%)
  between operations  1.95 us (3%)
    pallas_call x1, Pallas kernels, local(): pl.pallas_call(functools.partial(layer_kernel, n_wide, n_narrow, scale, s...  52.9 us
    pallas_call x1, Pallas kernels, local(): pl.pallas_call(finish_kernel, name='finish', out_shape=(shape(chunked, BF...  4.64 us

profile of v3, /device:TPU:0, one launch (start us, length us, event | category | flops | bytes accessed | tf_op | source)
XLA Modules:
  0.0 59.5 jit_solution(7699964176393181366)
XLA Ops:
  1.9 0.0 copy-start
  1.9 52.9 %layer.1 = (bf16[32,128,512]{2,1,0:T(8,128)(2,1)S(1)}, bf16[32,128,512]{2,1,0:T(8,128)(2,1)S(1)}, bf16[4,256,512]{2,1,0:T(8,128)(2,1)S(1)}, bf16[2,8,4,64,64]{4,3,2,1,0:T(8,128)(2,1)S(1)}, f32[1,512]{1,0:T(1,128)S(1)}) custom-call(s32[1,4,256]{2,1,0:T(4,128)} %idx_ref.3, s32[1,96]{1,0:T(1,128)} %row_ref.1, s32[1,96]{1,0:T(1,128)} %col_ref.1, ...), custom_call_target="tpu_custom_call" | custom-call | tf_op jit(solution)/shard_map/layer/pallas_call | solution.py:608
  54.9 0.0 copy-done
  54.9 4.6 %finish.1 = (bf16[16,256,512]{2,1,0:T(8,128)(2,1)}, bf16[32,128,512]{2,1,0:T(8,128)(2,1)}, f32[512,512]{1,0:T(8,128)}, f32[1,512]{1,0:T(1,128)}) custom-call(s32[1,4,256]{2,1,0:T(4,128)S(1)} %copy-done, bf16[16,256,512]{2,1,0:T(8,128)(2,1)S(1)} %bitcast.7, bf16[4,256,512]{2,1,0:T(8,128)(2,1)S(1)} %get-tuple-element.14.incoming, ...), custom_call_target="tpu_custom_call" | custom-call | tf_op jit(solution)/shard_map/finish/pallas_call | solution.py:666
Async XLA Ops:
  1.9 52.9 %copy-start = (s32[1,4,256]{2,1,0:T(4,128)S(1)}, s32[1,4,256]{2,1,0:T(4,128)}, u32[]{:S(2)}) copy-start(s32[1,4,256]{2,1,0:T(4,128)} %idx_ref.3) | copy-start | bytes 12292

commit v4 on v3

--- a/solution.py
+++ b/solution.py
@@ -164,7 +164,7 @@
     count = idx_ref.shape[2]
     per = count // side
     slab, across = rs_wide.shape[2:]
-    part_width = rs_narrow.shape[3]
+    lines = rs_narrow.shape[2]
     keep_to = nodes_live[0]
 
     loads = [
@@ -174,8 +174,7 @@
         pltpu.make_async_copy(w_hbm, w_ref, load.at[3]),
         pltpu.make_async_copy(grad_hbm, grad, load.at[4]),
     ]
-    for fetch in loads:
-        fetch.start()
+    loads[0].start()
 
     def wide_peer(d):
         return (lax.rem(w + d, n_wide), n)
@@ -205,6 +204,8 @@
     wsum[...] = jnp.zeros_like(wsum)
     bsum[...] = jnp.zeros_like(bsum)
     loads[0].wait()
+    for fetch in loads[1:3]:
+        fetch.start()
     span = half * side
     lane = lax.broadcasted_iota(jnp.int32, (count, 128), 1).astype(F32)
 
@@ -228,6 +229,9 @@
         @pl.when(there)
         def _():
             halo_copy(packed, landing, send, recv, k, target).start()
+
+    for fetch in loads[3:]:
+        fetch.start()
 
     def kept(block, blocks=1):
         at = lax.broadcasted_iota(jnp.int32, (blocks * side, width), 0)
@@ -341,7 +345,7 @@
         for d in range(1, n_wide):
             total = total + rs_wide[h, d].astype(F32)
         for j in range(n_narrow):
-            part[h, j] = total[:, j * part_width : (j + 1) * part_width].astype(BF)
+            part[h, j] = total[j * lines : (j + 1) * lines].astype(BF)
         copies = []
         for d in range(1, n_narrow):
             peer = narrow_peer(d)
@@ -529,7 +533,7 @@
     part_give,
 ):
     half, chunk, width = grad.shape
-    parts, n_wide, n_narrow, slab, part_width = ag_wide.shape
+    parts, n_wide, n_narrow, lines, across = ag_wide.shape
     moves = [
         pltpu.make_async_copy(out_ref, out_hbm, give.at[0]),
         pltpu.make_async_copy(
@@ -539,9 +543,11 @@
     ]
     for c in moves:
         c.start()
-    for i in range(n_wide):
-        line = [ag_wide[h, i, j] for h in range(parts) for j in range(n_narrow)]
-        wg[pl.ds(i * slab, slab), :] = jnp.concatenate(line, 1).astype(F32)
+    for h in range(parts):
+        for i in range(n_wide):
+            for j in range(n_narrow):
+                at = pl.ds((i * n_narrow + j) * lines, lines)
+                wg[at, h * across : (h + 1) * across] = ag_wide[h, i, j].astype(F32)
     moves.append(pltpu.make_async_copy(wg, w_hbm, give.at[3]))
     moves[3].start()
     merged = incoming[...].reshape(-1, width)
@@ -599,7 +605,7 @@
     slab = width // n_wide
     parts = 2
     across = width // parts
-    part_width = across // n_narrow
+    lines = slab // n_narrow
     scale = 1.0 / math.sqrt(nodes * n_wide * n_narrow)
     step = 4
     chunk = 2 * side
@@ -612,7 +618,7 @@
             pltpu.VMEM(blocked, BF),
             pltpu.VMEM(blocked, BF),
             pltpu.VMEM((sides, halo, width), BF),
-            pltpu.VMEM((parts, n_wide, n_narrow, slab, part_width), BF),
+            pltpu.VMEM((parts, n_wide, n_narrow, lines, across), BF),
             pltpu.VMEM((1, width), F32),
         ),
         in_specs=[vm, vm, vm, sm, sm, vm, hb, hb, hb, hb],
@@ -633,9 +639,9 @@
             pltpu.VMEM((8, width), F32),
             pltpu.VMEM((1, width), F32),
             pltpu.VMEM((parts, n_wide, slab, across), BF),
-            pltpu.VMEM((parts, n_narrow, slab, part_width), BF),
-            pltpu.VMEM((parts, n_narrow, slab, part_width), BF),
-            pltpu.VMEM((parts, n_narrow, slab, part_width), BF),
+            pltpu.VMEM((parts, n_narrow, lines, across), BF),
+            pltpu.VMEM((parts, n_narrow, lines, across), BF),
+            pltpu.VMEM((parts, n_narrow, lines, across), BF),
             pltpu.VMEM((n_wide, 1, width), F32),
             pltpu.VMEM((1, width), F32),
             pltpu.VMEM((n_narrow, 1, width), F32),

time: 59.7 us -> 54 us (0.905)
  Pallas kernels: 57.6 us -> 51.8 us
    pallas_call x1, Pallas kernels: 52.9 us -> 47.3 us  [local(): pl.pallas_call(functools.partial(layer_kernel, n_wide, n_narrow, scale, s...]
where the time goes in v4:
time: 54 us; the launch traced here: 53.8 us
  Pallas kernels  51.8 us (96%)
  between operations  1.95 us (4%)
    pallas_call x1, Pallas kernels, local(): pl.pallas_call(functools.partial(layer_kernel, n_wide, n_narrow, scale, s...  47.3 us
    pallas_call x1, Pallas kernels, local(): pl.pallas_call(finish_kernel, name='finish', out_shape=(shape(chunked, BF...  4.54 us

profile of v4, /device:TPU:0, one launch (start us, length us, event | category | flops | bytes accessed | tf_op | source)
XLA Modules:
  0.0 53.8 jit_solution(7285609548602942232)
XLA Ops:
  1.9 0.0 copy-start
  1.9 47.3 %layer.1 = (bf16[32,128,512]{2,1,0:T(8,128)(2,1)S(1)}, bf16[32,128,512]{2,1,0:T(8,128)(2,1)S(1)}, bf16[4,256,512]{2,1,0:T(8,128)(2,1)S(1)}, bf16[2,8,4,16,256]{4,3,2,1,0:T(8,128)(2,1)S(1)}, f32[1,512]{1,0:T(1,128)S(1)}) custom-call(s32[1,4,256]{2,1,0:T(4,128)} %idx_ref.3, s32[1,96]{1,0:T(1,128)} %row_ref.1, s32[1,96]{1,0:T(1,128)} %col_ref.1, ...), custom_call_target="tpu_custom_call" | custom-call | tf_op jit(solution)/shard_map/layer/pallas_call | solution.py:614
  49.2 0.0 copy-done
  49.2 4.5 %finish.1 = (bf16[16,256,512]{2,1,0:T(8,128)(2,1)}, bf16[32,128,512]{2,1,0:T(8,128)(2,1)}, f32[512,512]{1,0:T(8,128)}, f32[1,512]{1,0:T(1,128)}) custom-call(s32[1,4,256]{2,1,0:T(4,128)S(1)} %copy-done, bf16[16,256,512]{2,1,0:T(8,128)(2,1)S(1)} %bitcast.7, bf16[4,256,512]{2,1,0:T(8,128)(2,1)S(1)} %get-tuple-element.14.incoming, ...), custom_call_target="tpu_custom_call" | custom-call | tf_op jit(solution)/shard_map/finish/pallas_call | solution.py:672
Async XLA Ops:
  1.9 47.3 %copy-start = (s32[1,4,256]{2,1,0:T(4,128)S(1)}, s32[1,4,256]{2,1,0:T(4,128)}, u32[]{:S(2)}) copy-start(s32[1,4,256]{2,1,0:T(4,128)} %idx_ref.3) | copy-start | bytes 12292

commit v5 on v4

--- a/solution.py
+++ b/solution.py
@@ -27,12 +27,14 @@
     )
 
 
-def halo_copy(src, dst, send, recv, k, target):
+def halo_copy(src, dst, send, recv, k, h, target):
+    columns = src.shape[2] // 2
+    at = pl.ds(h * columns, columns)
     return pltpu.make_async_remote_copy(
-        src_ref=src.at[k],
-        dst_ref=dst.at[k ^ 1],
-        send_sem=send.at[k],
-        recv_sem=recv.at[k ^ 1],
+        src_ref=src.at[k, :, at],
+        dst_ref=dst.at[k ^ 1, :, at],
+        send_sem=send.at[k, h],
+        recv_sem=recv.at[k ^ 1, h],
         device_id=target,
         device_id_type=MESH,
     )
@@ -228,7 +230,8 @@
 
         @pl.when(there)
         def _():
-            halo_copy(packed, landing, send, recv, k, target).start()
+            for h in range(2):
+                halo_copy(packed, landing, send, recv, k, h, target).start()
 
     for fetch in loads[3:]:
         fetch.start()
@@ -259,22 +262,32 @@
         return carry
 
     lax.fori_loop(0, row_blocks // unroll, leading, 0)
-    for k in (1, 0, 2, 3):
-        there, target = near[k]
-
-        @pl.when(there)
-        def _():
-            halo_copy(packed, landing, send, recv, k, target).wait_send()
-            halo_copy(packed, landing, send, recv, k ^ 1, target).wait_recv()
-            ext[pl.ds(row_blocks + k * per, per)] = landing[k].reshape(per, side, width)
-
-    def following(t, carry):
-        for u in range(unroll):
-            k = t * unroll + u
-            run[k] = run[table[2, k]] + product(k)
-        return carry
-
-    lax.fori_loop(row_blocks // unroll, slots // unroll, following, 0)
+    def following(h):
+        columns = width // 2
+        at = slice(h * columns, (h + 1) * columns)
+        for k in (1, 0, 2, 3):
+            there, target = near[k]
+
+            @pl.when(there)
+            def _():
+                halo_copy(packed, landing, send, recv, k, h, target).wait_send()
+                halo_copy(packed, landing, send, recv, k ^ 1, h, target).wait_recv()
+                ext[pl.ds(row_blocks + k * per, per), :, at] = landing[k, :, at].reshape(
+                    per, side, columns
+                )
+
+        def body(t, carry):
+            for u in range(unroll):
+                k = t * unroll + u
+                run[k, :, at] = run[table[2, k], :, at] + jnp.dot(
+                    adj[table[0, k]], ext[table[1, k], :, at], preferred_element_type=F32
+                )
+            return carry
+
+        lax.fori_loop(row_blocks // unroll, slots // unroll, body, 0)
+
+    following(0)
+    following(1)
     loads[3].wait()
     loads[4].wait()
 
@@ -647,7 +660,7 @@
             pltpu.VMEM((n_narrow, 1, width), F32),
             dma((6,)),
         ]
-        + [dma((sides,))] * 2
+        + [dma((sides, 2))] * 2
         + [dma((sides, halo // side))] * 2
         + [dma((parts, n_wide))] * 2
         + [dma((parts, n_narrow))] * 4

time: 54 us -> 53.7 us (level)
  no operation moved by 1% of the time
where the time goes in v5:
time: 53.7 us; the launch traced here: 53.5 us
  Pallas kernels  51.6 us (96%)
  between operations  1.95 us (4%)
    pallas_call x1, Pallas kernels, local(): pl.pallas_call(functools.partial(layer_kernel, n_wide, n_narrow, scale, s...  47 us
    pallas_call x1, Pallas kernels, local(): pl.pallas_call(finish_kernel, name='finish', out_shape=(shape(chunked, BF...  4.54 us

profile of v5, /device:TPU:0, one launch (start us, length us, event | category | flops | bytes accessed | tf_op | source)
XLA Modules:
  0.0 53.5 jit_solution(18428479077766062532)
XLA Ops:
  1.9 0.0 copy-start
  1.9 47.0 %layer.1 = (bf16[32,128,512]{2,1,0:T(8,128)(2,1)S(1)}, bf16[32,128,512]{2,1,0:T(8,128)(2,1)S(1)}, bf16[4,256,512]{2,1,0:T(8,128)(2,1)S(1)}, bf16[2,8,4,16,256]{4,3,2,1,0:T(8,128)(2,1)S(1)}, f32[1,512]{1,0:T(1,128)S(1)}) custom-call(s32[1,4,256]{2,1,0:T(4,128)} %idx_ref.3, s32[1,96]{1,0:T(1,128)} %row_ref.1, s32[1,96]{1,0:T(1,128)} %col_ref.1, ...), custom_call_target="tpu_custom_call" | custom-call | tf_op jit(solution)/shard_map/layer/pallas_call | solution.py:627
  49.0 0.0 copy-done
  49.0 4.5 %finish.1 = (bf16[16,256,512]{2,1,0:T(8,128)(2,1)}, bf16[32,128,512]{2,1,0:T(8,128)(2,1)}, f32[512,512]{1,0:T(8,128)}, f32[1,512]{1,0:T(1,128)}) custom-call(s32[1,4,256]{2,1,0:T(4,128)S(1)} %copy-done, bf16[16,256,512]{2,1,0:T(8,128)(2,1)S(1)} %bitcast.7, bf16[4,256,512]{2,1,0:T(8,128)(2,1)S(1)} %get-tuple-element.14.incoming, ...), custom_call_target="tpu_custom_call" | custom-call | tf_op jit(solution)/shard_map/finish/pallas_call | solution.py:685
Async XLA Ops:
  1.9 47.1 %copy-start = (s32[1,4,256]{2,1,0:T(4,128)S(1)}, s32[1,4,256]{2,1,0:T(4,128)}, u32[]{:S(2)}) copy-start(s32[1,4,256]{2,1,0:T(4,128)} %idx_ref.3) | copy-start | bytes 12292
